TPU v7x, 32 devices: a whole 2x2x4 slice. The times are simulated.
32 devices in a mesh: seg: 8 (over z, core), bond: 4 (over y, x).
Axes of the slice: x: 2, y: 2, z: 4, core: 2. Of those that a mesh axis runs over, the one named last changes fastest.
Arguments:
- left_env: bfloat16 [8, 1024, 6, 1024], P('seg', 'bond'), may hold values from -0.1875 to 0.1875
- prev_left: bfloat16 [8, 1024, 1024], P('seg'), may hold values from -0.25 to 1.25
- cur_site: bfloat16 [8, 1024, 4, 1024], P('seg', 'bond'), may hold values from -6 to 6
- prev_site: bfloat16 [8, 1024, 4, 1024], P('seg', None, None, 'bond'), may hold values from -6 to 6
- hamiltonian: bfloat16 [8, 6, 6, 4, 4], P('seg'), may hold values from -1.25 to 1.25
- right_env: bfloat16 [8, 1024, 6, 1024], P('seg', 'bond'), may hold values from -0.078125 to 0.078125
- prev_right: bfloat16 [8, 1024, 1024], P('seg'), may hold values from -0.25 to 1.25
Outputs:
- new_site: bfloat16 [8, 1024, 4, 1024], P('seg', 'bond')
- center: float32 [8, 1024, 1024], P('seg', 'bond')
All inputs are finite; a program needn't handle non-finite values.
Results may differ from a plain program's by a relative error of at most 0.0054.
Values may be sent and summed in bfloat16 or wider, within the bound.
A program may use at most 128 MiB of HBM per device.

v0:
```python
import functools
import math

import jax
import jax.numpy as jnp
from jax import lax
from jax.experimental import pallas as pl
from jax.experimental.pallas import tpu as pltpu
from jax.sharding import PartitionSpec as P

PHYS = 4
MPOB = 6
BLOCK = 128
STRIP = 256
GROUP = 4
ROWS = 8
WAVES = 2


def shifted(block, axis, distance):
    devices = range(lax.axis_size(axis))
    route = [((i - distance) % len(devices), i) for i in devices]
    return lax.ppermute(block, axis, route)


def halves(x):
    high = x.astype(jnp.bfloat16)
    return high, (x - high.astype(jnp.float32)).astype(jnp.bfloat16)


def product(a, b, dims):
    a_high, a_low = halves(a)
    b_high, b_low = halves(b)

    def dot(x, y):
        return lax.dot_general(x, y, (dims, ((), ())), preferred_element_type=jnp.float32)

    return dot(a_high, b_high) + (dot(a_high, b_low) + dot(a_low, b_high))


def reduce_kernel(n, own_ref, out_ref, parts, total, send_sem, recv_sem, send_back, recv_back):
    me = lax.axis_index("bond")
    barrier = pltpu.get_barrier_semaphore()
    peers = [lax.rem(me + d, n) for d in range(1, n)]
    for peer in peers:
        pl.semaphore_signal(barrier, inc=1, device_id={"bond": peer})
    pl.semaphore_wait(barrier, n - 1)
    width = own_ref.shape[2] // WAVES
    waves = [pl.ds(w * width, width) for w in range(WAVES)]
    outward, back = [], []
    for w, lanes in enumerate(waves):
        outward.append([
            pltpu.make_async_remote_copy(
                src_ref=own_ref.at[peer, :, lanes],
                dst_ref=parts.at[d, :, lanes],
                send_sem=send_sem.at[w, d],
                recv_sem=recv_sem.at[w, d],
                device_id={"bond": peer},
            )
            for d, peer in enumerate(peers)
        ])
        for copy in outward[w]:
            copy.start()
    for w, lanes in enumerate(waves):
        for copy in outward[w]:
            copy.wait_recv()
        value = own_ref[me, :, lanes]
        for d in range(n - 1):
            value = value + parts[d, :, lanes]
        total[me, :, lanes] = value
        back.append([
            pltpu.make_async_remote_copy(
                src_ref=total.at[me, :, lanes],
                dst_ref=total.at[me, :, lanes],
                send_sem=send_back.at[w, d],
                recv_sem=recv_back.at[w, d],
                device_id={"bond": peer},
            )
            for d, peer in enumerate(peers)
        ])
        for copy in back[w]:
            copy.start()
    for w, lanes in enumerate(waves):
        for copy in back[w]:
            copy.wait_recv()
        out_ref[:, :, lanes] = total[:, :, lanes]
    for copies in outward + back:
        for copy in copies:
            copy.wait_send()


def summed(packed):
    n = lax.axis_size("bond")
    rows, width = packed.shape
    shape = (n, rows // n, width)
    return pl.pallas_call(
        functools.partial(reduce_kernel, n),
        out_shape=jax.ShapeDtypeStruct(shape, jnp.float32),
        in_specs=[pl.BlockSpec(memory_space=pltpu.VMEM)],
        out_specs=pl.BlockSpec(memory_space=pltpu.VMEM),
        scratch_shapes=[
            pltpu.VMEM((n - 1,) + shape[1:], jnp.float32),
            pltpu.VMEM(shape, jnp.float32),
        ]
        + [pltpu.SemaphoreType.DMA((WAVES, n - 1))] * 4,
        compiler_params=pltpu.CompilerParams(
            collective_id=0, has_side_effects=True, vmem_limit_bytes=24 * 2**20
        ),
        name="summed",
    )(packed.reshape(shape)).reshape(rows, width)


def eliminate(block, rows_ref):
    size = block.shape[0]
    lane = lax.broadcasted_iota(jnp.int32, (1, size), 1)
    rest = block
    top = 0
    for first in range(0, size, GROUP):
        start = first // 8 * 8
        rest, top = rest[start - top :], start
        at = first - top
        rows = [rest[at + q : at + q + 1, :] for q in range(GROUP)]
        columns = [
            jnp.broadcast_to(rest[:, first + q : first + q + 1], rest.shape) for q in range(GROUP)
        ]
        small = [[columns[r][at + p : at + p + 1, :] for r in range(GROUP)] for p in range(GROUP)]
        change = None
        for q in range(GROUP):
            rows_ref[pl.ds(first + q, 1), :] = rows[q]
            inverse = 1.0 / small[q][q]
            lead = jnp.where(lane == first + q, 1.0, rows[q])
            for p in range(q + 1, GROUP):
                factor = small[q][p] * inverse
                for r in range(p, GROUP):
                    small[p][r] = small[p][r] - factor * small[q][r]
                rows[p] = jnp.where(lane == first + q, 0.0, rows[p]) - factor * lead
                columns[p] = columns[p] - factor * columns[q]
            if first + GROUP < size:
                lead = jnp.where((lane > first + q) & (lane < first + GROUP), 0.0, lead)
                term = columns[q] * (inverse * lead)
                change = term if change is None else change + term
        if first + GROUP < size:
            rest = jnp.where((lane >= first) & (lane < first + GROUP), 0.0, rest) - change


def factor_kernel(packed_ref, upper_ref, inverse_ref, work, panel, rows_ref):
    size = work.shape[0]
    blocks = size // BLOCK
    offset = 0
    for start in range(0, size, STRIP):
        width = size - start
        work[start : start + STRIP, start:] = packed_ref[:, offset : offset + width]
        if start > 0:
            work[start : start + STRIP, :start] = jnp.zeros((STRIP, start), jnp.float32)
        offset += width
    row = lax.broadcasted_iota(jnp.int32, (BLOCK, BLOCK), 0)
    column = lax.broadcasted_iota(jnp.int32, (BLOCK, BLOCK), 1)
    full_column = lax.broadcasted_iota(jnp.int32, (BLOCK, size), 1)

    def step(k, carry):
        own = pl.ds(pl.multiple_of(k * BLOCK, BLOCK), BLOCK)
        eliminate(work[own, own], rows_ref)
        done = rows_ref[...]
        pivots = jnp.sum(jnp.where(row == column, done, 0.0), axis=1, keepdims=True)
        scale = lax.rsqrt(pivots)
        scaled = done * scale
        upper = jnp.where(row <= column, scaled, 0.0)
        inverse = jnp.where(row > column, scaled, jnp.where(row == column, scale, 0.0))
        panel[...] = product(inverse, work[own, :], ((1,), (0,)))
        whole = panel[...]
        upper_ref[own, :] = jnp.where(full_column >= (k + 1) * BLOCK, whole, 0.0)
        inverse_ref[own, :] = jnp.where(full_column < k * BLOCK, whole, 0.0)
        upper_ref[own, own] = upper
        inverse_ref[own, own] = inverse
        panel[:, own] = inverse
        right = panel[...]

        def update(i, carry):
            other = pl.ds(pl.multiple_of(i * BLOCK, BLOCK), BLOCK)
            work[other, own] = jnp.zeros((BLOCK, BLOCK), jnp.float32)
            work[other, :] -= product(panel[:, other], right, ((0,), (0,)))
            return carry

        lax.fori_loop(k + 1, blocks, update, 0)
        return carry

    lax.fori_loop(0, blocks, step, 0)


def factorize(packed, size):
    whole = jax.ShapeDtypeStruct((size, size), jnp.float32)
    return pl.pallas_call(
        factor_kernel,
        out_shape=(whole, whole),
        in_specs=[pl.BlockSpec(memory_space=pltpu.VMEM)],
        out_specs=[pl.BlockSpec(memory_space=pltpu.VMEM)] * 2,
        scratch_shapes=[
            pltpu.VMEM((size, size), jnp.float32),
            pltpu.VMEM((BLOCK, size), jnp.float32),
            pltpu.VMEM((BLOCK, BLOCK), jnp.float32),
        ],
        compiler_params=pltpu.CompilerParams(vmem_limit_bytes=40 * 2**20),
        name="factorize",
    )(packed)


def mix_kernel(parts, spread_ref, projected_ref, mixture_ref):
    width = projected_ref.shape[2] // PHYS
    spread = spread_ref[...]
    results = []
    for first in range(0, 2 * ROWS, ROWS):
        stack = jnp.concatenate(
            [
                projected_ref[u, first : first + ROWS, t * width : (t + 1) * width]
                for u in range(MPOB)
                for t in range(PHYS)
            ],
            axis=0,
        )
        high, low = halves(stack)
        results.append(
            jnp.dot(spread, high, preferred_element_type=jnp.float32)
            + jnp.dot(spread, low, preferred_element_type=jnp.float32)
        )
    for v in range(MPOB):
        for s in range(PHYS):
            at = (v * PHYS + s) * ROWS
            both = jnp.concatenate([one[at : at + ROWS, :] for one in results], axis=0)
            both = both.astype(jnp.bfloat16)
            part = width // parts
            for p in range(parts):
                start = (p * MPOB + v) * part
                mixture_ref[s, :, start : start + part] = both[:, p * part : (p + 1) * part]


def mixed(projected, coupling, parts):
    own_rows, width = projected.shape[1], projected.shape[2] // PHYS
    side = MPOB * PHYS * ROWS
    diagonal = jnp.eye(ROWS, dtype=coupling.dtype)
    turned = jnp.transpose(coupling, (1, 2, 0, 3))
    spread = turned[:, :, None, :, :, None] * diagonal[None, None, :, None, None, :]
    return pl.pallas_call(
        functools.partial(mix_kernel, parts),
        grid=(own_rows // (2 * ROWS),),
        out_shape=jax.ShapeDtypeStruct((PHYS, own_rows, MPOB * width), jnp.bfloat16),
        in_specs=[
            pl.BlockSpec((side, side), lambda i: (0, 0)),
            pl.BlockSpec((MPOB, 2 * ROWS, PHYS * width), lambda i: (0, i, 0)),
        ],
        out_specs=pl.BlockSpec((PHYS, 2 * ROWS, MPOB * width), lambda i: (0, i, 0)),
        compiler_params=pltpu.CompilerParams(vmem_limit_bytes=40 * 2**20),
        cost_estimate=pl.CostEstimate(
            flops=4 * side * MPOB * PHYS * own_rows * width,
            bytes_accessed=6 * MPOB * PHYS * own_rows * width,
            transcendentals=0,
        ),
        name="mixed",
    )(spread.reshape(side, side), projected)


def shards(left_env, prev_left, cur_site, prev_site, hamiltonian, right_env, prev_right):
    left_now, prev_now = shifted((left_env[0], prev_left[0]), "seg", 1)
    own_rows = left_now.shape[0]
    bond_width = left_now.shape[2]
    current = lax.all_gather(cur_site[0], "bond", axis=0, tiled=True)
    left_terms = jnp.transpose(left_now, (1, 0, 2)).reshape(MPOB * own_rows, bond_width)
    projected = jnp.dot(
        left_terms,
        current.reshape(bond_width, PHYS * bond_width),
        preferred_element_type=jnp.float32,
    ).reshape(MPOB, own_rows, PHYS * bond_width)
    parts = lax.axis_size("bond") if own_rows % 128 == 0 else 1
    mixture = mixed(projected, hamiltonian[0], parts)
    partial_value = jnp.einsum(
        "ab,bsc->asc", prev_now, prev_site[0], preferred_element_type=jnp.float32
    ).astype(jnp.bfloat16)
    second = jnp.einsum(
        "akc,cy->kay",
        lax.all_to_all(partial_value, "bond", split_axis=0, concat_axis=2, tiled=True),
        prev_right[0],
        preferred_element_type=jnp.float32,
    )
    flat_rows = own_rows * PHYS
    right_terms = jnp.transpose(right_env[0], (1, 0, 2))
    if parts > 1:
        right = lax.all_gather(
            right_terms.reshape(MPOB * own_rows, bond_width), "bond", axis=0, tiled=True
        )
    else:
        right = lax.all_gather(right_terms, "bond", axis=1, tiled=True)
    applied = jnp.dot(
        mixture.reshape(flat_rows, MPOB * bond_width),
        right.reshape(MPOB * bond_width, bond_width),
        preferred_element_type=jnp.float32,
    )
    target = 2.0 * applied - second.reshape(flat_rows, bond_width)
    strips = [
        jnp.dot(
            target[:, start : start + STRIP].T,
            target[:, start:],
            precision=lax.Precision.HIGH,
            preferred_element_type=jnp.float32,
        )
        for start in range(0, bond_width, STRIP)
    ]
    packed = summed(jnp.concatenate(strips, axis=1))
    upper, inverse = factorize(packed, bond_width)
    norming = math.sqrt(bond_width * PHYS)
    solved = lax.dot_general(
        target,
        inverse,
        (((1,), (1,)), ((), ())),
        precision=lax.Precision.HIGH,
        preferred_element_type=jnp.float32,
    )
    new_site = (solved * norming).astype(jnp.bfloat16).reshape(PHYS, own_rows, bond_width)
    new_site = jnp.transpose(new_site, (1, 0, 2))[None]
    offset = lax.axis_index("bond") * own_rows
    center = lax.dynamic_slice_in_dim(upper, offset, own_rows, 0) / norming
    return (new_site, center[None])


def solution(mesh):
    return jax.shard_map(
        shards,
        mesh=mesh,
        in_specs=(
            P("seg", "bond", None, None),
            P("seg", None, None),
            P("seg", "bond", None, None),
            P("seg", None, None, "bond"),
            P("seg", None, None, None, None),
            P("seg", "bond", None, None),
            P("seg", None, None),
        ),
        out_specs=(P("seg", "bond", None, None), P("seg", "bond", None)),
        check_vma=False,
    )
```

profile of v0, /device:TPU:0, one launch (start us, length us, event | category | flops | bytes accessed | tf_op | source)
XLA Modules:
  0.0 392.1 jit_solution(15401734456700709113)
XLA Ops:
  9.2 2.7 collective-permute-start
  11.9 25.3 %collective-permute-done.1 = bf16[1024,1024]{1,0:T(8,128)(2,1)S(1)} collective-permute-done((bf16[1024,1024]{1,0:T(8,128)(2,1)}, bf16[1024,1024]{1,0:T(8,128)(2,1)S(1)}, u32[]{:S(2)}, u32[]{:S(2)}) %collective-permute-start.1) | collective-permute-done | bytes 2097184 | tf_op jit(solution)/shard_map/ppermute | solution.py:23
  37.2 2.3 fusion.11
  39.5 2.9 copy.17
  42.4 4.8 %all-to-all-start = ((bf16[1024,4,256]{2,1,0:T(4,128)(2,1)}), bf16[1024,4,256]{2,1,0:T(4,128)(2,1)}, u32[]{:S(2)}, u32[]{:S(2)}) async-start(bf16[1024,4,256]{2,1,0:T(4,128)(2,1)} %copy.17), calls=%async_computation | async-start | bytes 4194304 | tf_op jit(solution)/shard_map/all_to_all | solution.py:279
  49.0 31.6 %all-to-all-done = bf16[1024,4,256]{2,1,0:T(4,128)(2,1)} async-done(((bf16[1024,4,256]{2,1,0:T(4,128)(2,1)}), bf16[1024,4,256]{2,1,0:T(4,128)(2,1)}, u32[]{:S(2)}, u32[]{:S(2)}) %all-to-all-start) | async-done | bytes 2097184 | tf_op jit(solution)/shard_map/all_to_all | solution.py:279
  80.6 4.5 %copy.29 = bf16[4,256,4,256]{3,0,1,2:T(4,128)(2,1)} copy(bf16[4,256,4,256]{3,2,1,0:T(4,128)(2,1)} %bitcast.12) | data formatting | bytes 4194304 | tf_op jit(solution)/shard_map/all_to_all | solution.py:279
  85.1 4.4 %all_to_all.16 = bf16[256,4,1024]{2,0,1:T(8,128)(2,1)} reshape(bf16[256,4,4,256]{3,2,0,1:T(4,128)(2,1)} %bitcast.58) | data formatting | bytes 4194304 | tf_op jit(solution)/shard_map/all_to_all | solution.py:279
  89.5 6.5 %fusion.6 = f32[256,4,1024]{2,0,1:T(8,128)} fusion(bf16[256,4,1024]{2,0,1:T(8,128)(2,1)} %all_to_all.16, bf16[1,1024,1024]{2,1,0:T(8,128)(2,1)} %param.13), kind=kOutput, calls=%fused_computation.9 | convolution fusion | flops 2147483648 | bytes 8388608 | tf_op jit(solution)/shard_map/akc,cy->kay/dot_general | solution.py:277
  96.0 19.5 %all-gather.6.cloned.1.call-done = bf16[1,1024,4,1024]{3,2,0,1:T(4,128)(2,1)} async-done(((bf16[1,256,4,1024]{3,2,0,1:T(4,128)(2,1)}), bf16[1,1024,4,1024]{3,2,0,1:T(4,128)(2,1)}) %all-gather.6.cloned.1.call-update) | async-done | bytes 8388624 | tf_op jit(solution)/shard_map/all_gather | solution.py:265
  115.5 14.7 %reshape.51 = bf16[1024,4096,1]{1,0,2:T(8,128)(2,1)} reshape(bf16[1,1024,4,1024]{3,2,0,1:T(4,128)(2,1)} %all-gather.6.cloned.1.call-done) | data formatting | bytes 16777216 | tf_op jit(solution)/shard_map/reshape | solution.py:269
  130.2 21.2 %fusion.2.projected_ref = f32[6,256,4096]{2,1,0:T(8,128)} fusion(bf16[1024,4096,1]{1,0,2:T(8,128)(2,1)} %reshape.51, bf16[256,6,1024]{2,0,1:T(8,128)(2,1)} %collective-permute-done), kind=kOutput, calls=%fused_computation.4 | convolution fusion | flops 12884901888 | bytes 36700160 | tf_op jit(solution)/shard_map/dot_general | solution.py:267
  151.5 17.9 %mixed.1 = bf16[4,256,6144]{2,1,0:T(8,128)(2,1)S(1)} custom-call(bf16[192,192]{1,0:T(8,128)(2,1)S(1)} %mul.35.spread_ref, f32[6,256,4096]{2,1,0:T(8,128)} %fusion.2.projected_ref), custom_call_target="tpu_custom_call" | custom-call | flops 4831838208 | bytes 37748736 | tf_op jit(solution)/shard_map/mixed/pallas_call | solution.py:242
  169.4 5.9 %copy-done.2 = bf16[4,256,6144]{2,1,0:T(8,128)(2,1)} copy-done((bf16[4,256,6144]{2,1,0:T(8,128)(2,1)}, bf16[4,256,6144]{2,1,0:T(8,128)(2,1)S(1)}, u32[]{:S(2)}) %copy-start.2) | copy-done | bytes 12582936
  175.3 63.9 %all-gather.4.cloned.1.call-done = bf16[6144,1024]{1,0:T(8,128)(2,1)} async-done(((bf16[1536,1024]{1,0:T(8,128)(2,1)}), bf16[6144,1024]{1,0:T(8,128)(2,1)}) %all-gather.4.cloned.1.call-update) | async-done | bytes 12582928 | tf_op jit(solution)/shard_map/all_gather | solution.py:286
  239.2 19.1 %bitcast_subtract_fusion = f32[1024,1024]{1,0:T(8,128)S(1)} fusion(f32[256,4,1024]{2,0,1:T(8,128)} %fusion.6, bf16[1024,6144]{1,0:T(8,128)(2,1)} %bitcast.55, bf16[6144,1024]{1,0:T(8,128)(2,1)} %all-gather.4.cloned.1.call-done), kind=kOutput, calls=%fused_computation | convolution fusion | flops 12886999040 | bytes 33554432 | tf_op jit(solution)/shard_map/dot_general | solution.py:291
  258.3 2.0 fusion.20
  260.3 1.6 fusion
  261.9 1.0 fusion.4
  264.2 59.8 %summed.1 = f32[4,64,2560]{2,1,0:T(8,128)S(1)} custom-call(f32[4,64,2560]{2,1,0:T(8,128)S(1)} %bitcast.56), custom_call_target="tpu_custom_call" | custom-call | tf_op jit(solution)/shard_map/summed/pallas_call | solution.py:96
  324.0 50.2 %factorize.1 = (f32[1024,1024]{1,0:T(8,128)S(1)}, f32[1024,1024]{1,0:T(8,128)S(1)}) custom-call(f32[256,2560]{1,0:T(8,128)S(1)} %bitcast.57), custom_call_target="tpu_custom_call" | custom-call | tf_op jit(solution)/shard_map/factorize/pallas_call | solution.py:192
  374.2 7.0 %multiply_convert_fusion = bf16[1024,1024]{1,0:T(8,128)(2,1)S(1)} fusion(f32[1024,1024]{1,0:T(8,128)S(1)} %bitcast_subtract_fusion, f32[1024,1024]{1,0:T(8,128)S(1)} %get-tuple-element.4), kind=kOutput, calls=%fused_computation.1 | convolution fusion | flops 6444548096 | bytes 10485760 | tf_op jit(solution)/shard_map/dot_general | solution.py:309
  381.2 2.9 copy.28
  384.1 1.1 multiply_bitcast_fusion
  (19 shorter events, 5.0 us)
Async XLA Ops:
  7.2 30.0 %copy-start = (bf16[1,1024,4,256]{3,2,1,0:T(4,128)(2,1)S(1)}, bf16[1,1024,4,256]{3,2,1,0:T(4,128)(2,1)}, u32[]{:S(2)}) copy-start(bf16[1,1024,4,256]{3,2,1,0:T(4,128)(2,1)} %param.10) | copy-start | bytes 6291460
  7.2 108.3 %all-gather.6.cloned.1.call-start = ((), (), s32[]{:S(2)}) async-start(), calls=%async_computation.2 | async-start | bytes 10485760 | tf_op jit(solution)/shard_map/all_gather | solution.py:265
  7.9 231.3 %all-gather.4.cloned.1.call-start = ((), (), s32[]{:S(2)}) async-start(), calls=%async_computation.1 | async-start | bytes 15728640 | tf_op jit(solution)/shard_map/all_gather | solution.py:286
  8.7 28.5 %collective-permute-start.1 = (bf16[1024,1024]{1,0:T(8,128)(2,1)}, bf16[1024,1024]{1,0:T(8,128)(2,1)S(1)}, u32[]{:S(2)}, u32[]{:S(2)}) collective-permute-start(bf16[1024,1024]{1,0:T(8,128)(2,1)} %bitcast.65), channel_id=1, source_target_pairs={{28,0},{0,4},{4,8},{8,12},{12,16},{16,20},{20,24},{24,28},{29,1},{... | collective-permute-start | bytes 6291464 | tf_op jit(solution)/shard_map/ppermute | solution.py:23
  9.2 121.0 %collective-permute-start = (bf16[256,6,1024]{2,0,1:T(8,128)(2,1)}, bf16[256,6,1024]{2,0,1:T(8,128)(2,1)}, u32[]{:S(2)}, u32[]{:S(2)}) collective-permute-start(bf16[256,6,1024]{2,0,1:T(8,128)(2,1)} %bitcast.64), channel_id=1, source_target_pairs={{28,0},{0,4},{4,8},{8,12},{12,16},{16,20},{20,24},{24,28},{29,1},{... | collective-permute-start | bytes 9437192 | tf_op jit(solution)/shard_map/ppermute | solution.py:23
  42.4 4.8 %copy-start.3 = (bf16[1,6,6,4,4]{2,4,3,1,0:T(4,128)(2,1)S(1)}, bf16[1,6,6,4,4]{2,4,3,1,0:T(4,128)(2,1)}, u32[]{:S(2)}) copy-start(bf16[1,6,6,4,4]{2,4,3,1,0:T(4,128)(2,1)} %param.11) | copy-start | bytes 3460
  42.4 38.1 %all-to-all-start = ((bf16[1024,4,256]{2,1,0:T(4,128)(2,1)}), bf16[1024,4,256]{2,1,0:T(4,128)(2,1)}, u32[]{:S(2)}, u32[]{:S(2)}) async-start(bf16[1024,4,256]{2,1,0:T(4,128)(2,1)} %copy.17), calls=%async_computation | async-start | bytes 4194304 | tf_op jit(solution)/shard_map/all_to_all | solution.py:279
  169.3 6.0 %copy-start.2 = (bf16[4,256,6144]{2,1,0:T(8,128)(2,1)}, bf16[4,256,6144]{2,1,0:T(8,128)(2,1)S(1)}, u32[]{:S(2)}) copy-start(bf16[4,256,6144]{2,1,0:T(8,128)(2,1)S(1)} %mixed.1) | copy-start | bytes 37748740
  381.2 4.0 %copy-start.1 = (bf16[1,1024,4,256]{3,2,1,0:T(4,128)(2,1)S(1)}, bf16[1,1024,4,256]{3,2,1,0:T(4,128)(2,1)}, u32[]{:S(2)}) copy-start(bf16[1,1024,4,256]{3,2,1,0:T(4,128)(2,1)} %param.10) | copy-start | bytes 6291460
Sparse Core Ops, SparseCore 0:
  9.8 105.6 all-gather.5
  117.4 121.8 all-gather.3
where the time goes:
time: 393 us; the launch traced here: 392 us
  waiting for transfers between devices  142 us (36%)
  Pallas kernels  128 us (33%)
  matrix products  61.7 us (16%)
  local copies, waits for them, and re-layouts  36.6 us (9%)
  between operations  14.2 us (4%)
  starting transfers between devices  8.05 us (2%)
    all_gather x1, waiting for transfers between devices, shards(): lax.all_gather(right_terms.reshape(MPOB * own_rows, bond_width), 'bond',...  63.9 us
    pallas_call x1, Pallas kernels, summed(): pl.pallas_call(functools.partial(reduce_kernel, n), out_shape=jax.ShapeDt...  59.8 us
    pallas_call x1, Pallas kernels, factorize(): pl.pallas_call(factor_kernel, out_shape=(whole, whole), in_specs=[pl.Bloc...  50.2 us
    all_to_all x1, waiting for transfers between devices, shards(): lax.all_to_all(partial_value, 'bond', split_axis=0, concat_axis=2, tiled=...  31.6 us
    ppermute x2, waiting for transfers between devices, shifted(): return lax.ppermute(block, axis, route)  25.3 us
    dot_general x1, matrix products, shards(): jnp.dot(left_terms, current.reshape(bond_width, PHYS * bond_width), prefe...  21.2 us
    all_gather x1, waiting for transfers between devices, shards(): current = lax.all_gather(cur_site[0], 'bond', axis=0, tiled=True)  19.5 us
    dot_general x1, matrix products, shards(): jnp.dot(mixture.reshape(flat_rows, MPOB * bond_width), right.reshape(MPOB...  19.1 us
  transfers between devices with their start and end apart: 5, of which 4 were waited for; matrix products, arithmetic and copies ran while one was open for 14% of the time, Pallas kernels for 5%

commit v1 on v0

--- a/solution.py
+++ b/solution.py
@@ -15,12 +15,7 @@
 GROUP = 4
 ROWS = 8
 WAVES = 2
-
-
-def shifted(block, axis, distance):
-    devices = range(lax.axis_size(axis))
-    route = [((i - distance) % len(devices), i) for i in devices]
-    return lax.ppermute(block, axis, route)
+CHUNKS = 4
 
 
 def halves(x):
@@ -217,10 +212,8 @@
             ],
             axis=0,
         )
-        high, low = halves(stack)
         results.append(
-            jnp.dot(spread, high, preferred_element_type=jnp.float32)
-            + jnp.dot(spread, low, preferred_element_type=jnp.float32)
+            jnp.dot(spread, stack.astype(jnp.bfloat16), preferred_element_type=jnp.float32)
         )
     for v in range(MPOB):
         for s in range(PHYS):
@@ -250,7 +243,7 @@
         out_specs=pl.BlockSpec((PHYS, 2 * ROWS, MPOB * width), lambda i: (0, i, 0)),
         compiler_params=pltpu.CompilerParams(vmem_limit_bytes=40 * 2**20),
         cost_estimate=pl.CostEstimate(
-            flops=4 * side * MPOB * PHYS * own_rows * width,
+            flops=2 * side * MPOB * PHYS * own_rows * width,
             bytes_accessed=6 * MPOB * PHYS * own_rows * width,
             transcendentals=0,
         ),
@@ -258,42 +251,90 @@
     )(spread.reshape(side, side), projected)
 
 
+def minor_size(n):
+    return max(d for d in range(1, n + 1) if n % d == 0 and d * d <= n)
+
+
+def sent(block, hop, major, minor):
+    segments, n = lax.axis_size("seg"), lax.axis_size("bond")
+    q = minor_size(n)
+    p = n // q
+    route = []
+    for k in range(segments):
+        for m in range(p):
+            for r in range(q):
+                source = (k - hop) % segments * n + (m + major) % p * q + (r + minor) % q
+                route.append((source, k * n + m * q + r))
+    return lax.ppermute(block, ("seg", "bond"), route)
+
+
+def blocks_of(array, indices, size, axis):
+    pieces = [lax.dynamic_slice_in_dim(array, j * size, size, axis) for j in indices]
+    return pieces[0] if len(pieces) == 1 else jnp.concatenate(pieces, axis=axis)
+
+
 def shards(left_env, prev_left, cur_site, prev_site, hamiltonian, right_env, prev_right):
-    left_now, prev_now = shifted((left_env[0], prev_left[0]), "seg", 1)
-    own_rows = left_now.shape[0]
-    bond_width = left_now.shape[2]
-    current = lax.all_gather(cur_site[0], "bond", axis=0, tiled=True)
-    left_terms = jnp.transpose(left_now, (1, 0, 2)).reshape(MPOB * own_rows, bond_width)
+    n = lax.axis_size("bond")
+    q = minor_size(n)
+    p = n // q
+    index = lax.axis_index("bond")
+    major, minor = index // q, index % q
+    own = left_env.shape[1]
+    bond = left_env.shape[3]
+    wide, tall = q * own, p * own
+
+    def at(m, r):
+        return lax.rem(m, p) * q + lax.rem(r, q)
+
+    current = jnp.zeros((bond, PHYS * wide), jnp.bfloat16)
+    for dm in range(p):
+        for dr in range(q):
+            m, r = major + p - dm, minor + q - dr
+            columns = [at(m, r + d) for d in range(q)]
+            block = blocks_of(cur_site[0], columns, own, 2).reshape(own, PHYS * wide)
+            if dm or dr:
+                block = sent(block, 0, dm, dr)
+            current = lax.dynamic_update_slice_in_dim(
+                current, block, at(major + dm, minor + dr) * own, 0
+            )
+    left_own = jnp.transpose(left_env[0], (1, 0, 2))
+    left = jnp.concatenate([sent(left_own, 1, d, 0) for d in range(p)], axis=1)
+    prev_now = sent(prev_left[0], 1, 0, 0)
+    right_own = jnp.transpose(right_env[0], (1, 0, 2))
+    right = [right_own] + [sent(right_own, 0, 0, d) for d in range(1, q)]
+    parts = q if own % 128 == 0 else 1
+    right = jnp.concatenate(right, axis=0 if parts == q else 1)
+
+    partial_value = jnp.einsum(
+        "ab,bsc->sac", prev_now, prev_site[0], preferred_element_type=jnp.float32
+    ).astype(jnp.bfloat16)
+    pieces = []
+    for d in range(q):
+        rows = [at(major + e, minor + q - d) for e in range(p)]
+        piece = blocks_of(partial_value, rows, own, 1)
+        pieces.append(sent(piece, 0, 0, d) if d else piece)
+    partial_value = jnp.concatenate(pieces, axis=2).reshape(PHYS * tall, wide)
+    prev_rows = blocks_of(prev_right[0], [at(major, minor + d) for d in range(q)], own, 0)
+
     projected = jnp.dot(
-        left_terms,
-        current.reshape(bond_width, PHYS * bond_width),
-        preferred_element_type=jnp.float32,
-    ).reshape(MPOB, own_rows, PHYS * bond_width)
-    parts = lax.axis_size("bond") if own_rows % 128 == 0 else 1
-    mixture = mixed(projected, hamiltonian[0], parts)
-    partial_value = jnp.einsum(
-        "ab,bsc->asc", prev_now, prev_site[0], preferred_element_type=jnp.float32
-    ).astype(jnp.bfloat16)
-    second = jnp.einsum(
-        "akc,cy->kay",
-        lax.all_to_all(partial_value, "bond", split_axis=0, concat_axis=2, tiled=True),
-        prev_right[0],
-        preferred_element_type=jnp.float32,
-    )
-    flat_rows = own_rows * PHYS
-    right_terms = jnp.transpose(right_env[0], (1, 0, 2))
-    if parts > 1:
-        right = lax.all_gather(
-            right_terms.reshape(MPOB * own_rows, bond_width), "bond", axis=0, tiled=True
-        )
-    else:
-        right = lax.all_gather(right_terms, "bond", axis=1, tiled=True)
-    applied = jnp.dot(
-        mixture.reshape(flat_rows, MPOB * bond_width),
-        right.reshape(MPOB * bond_width, bond_width),
-        preferred_element_type=jnp.float32,
-    )
-    target = 2.0 * applied - second.reshape(flat_rows, bond_width)
+        left.reshape(MPOB * tall, bond), current, preferred_element_type=jnp.float32
+    ).reshape(MPOB, tall, PHYS * wide)
+    mixture = mixed(projected, hamiltonian[0], parts).reshape(PHYS * tall, MPOB * wide)
+    right = right.reshape(MPOB * wide, bond)
+    columns = bond // CHUNKS
+    target = []
+    for j in range(CHUNKS):
+        lanes = slice(j * columns, (j + 1) * columns)
+        applied = jnp.dot(mixture, right[:, lanes], preferred_element_type=jnp.float32)
+        second = jnp.dot(partial_value, prev_rows[:, lanes], preferred_element_type=jnp.float32)
+        both = (2.0 * applied - second).reshape(PHYS, p, own, columns)
+        total = both[:, 0]
+        for d in range(1, p):
+            other = both[:, d].astype(jnp.bfloat16)
+            total = total + sent(other, 0, p - d, 0).astype(jnp.float32)
+        target.append(total.reshape(PHYS * own, columns))
+    target = jnp.concatenate(target, axis=1)
+    own_rows, bond_width = own, bond
     strips = [
         jnp.dot(
             target[:, start : start + STRIP].T,

time: 393 us -> 365 us (0.929)
  waiting for transfers between devices: 142 us -> 117 us
  Pallas kernels: 128 us -> 106 us
  matrix products: 61.7 us -> 76.7 us
  between operations: 14.2 us -> 1.18 us
  other arithmetic: 1.98 us -> 14.8 us
  local copies, waits for them, and re-layouts: 36.6 us -> 28 us
  starting transfers between devices: 8.05 us -> 15.6 us
    ppermute x2 -> x12, waiting for transfers between devices: 25.3 us -> 117 us  [sent(): return lax.ppermute(block, ('seg', 'bond'), route)]
    all_gather x2 -> x0, waiting for transfers between devices: 83.5 us -> none  [the longest x1 63.9 us: shards(): lax.all_gather(right_terms.reshape(MPOB * own_rows, bond_width), 'bond',...]
    all_to_all x1 -> x0, waiting for transfers between devices: 31.6 us -> none  [shards(): lax.all_to_all(partial_value, 'bond', split_axis=0, concat_axis=2, tiled=...]
    pallas_call x1, Pallas kernels: 59.8 us -> 32.5 us  [summed(): pl.pallas_call(functools.partial(reduce_kernel, n), out_shape=jax.ShapeDt...]
    dot_general x4 -> x10, matrix products: 49.1 us -> 64.2 us  [the longest x1 32.1 us: shards(): jnp.dot(left.reshape(MPOB * tall, bond), current, preferred_element_type=...]
    reshape x1 -> x0, local copies, waits for them, and re-layouts: 14.7 us -> none  [shards(): current.reshape(bond_width, PHYS * bond_width)]
    concatenate x0 -> x4, other arithmetic: none -> 12.4 us  [the longest x1 6.03 us: shards(): right = jnp.concatenate(right, axis=0 if parts == q else 1)]
    ppermute x2 -> x12, starting transfers between devices: 3.22 us -> 15.6 us  [sent(): return lax.ppermute(block, ('seg', 'bond'), route)]
  transfers between devices with their start and end apart: 5 -> 12, of which waited for: 4 -> 4; matrix products, arithmetic and copies ran while one was open for 14% -> 25% of each run, Pallas kernels for 5% -> 7%
where the time goes in v1:
time: 365 us; the launch traced here: 360 us
  waiting for transfers between devices  117 us (32%)
  Pallas kernels  106 us (29%)
  matrix products  76.7 us (21%)
  local copies, waits for them, and re-layouts  28 us (8%)
  starting transfers between devices  15.6 us (4%)
  other arithmetic  14.8 us (4%)
    ppermute x12, waiting for transfers between devices, sent(): return lax.ppermute(block, ('seg', 'bond'), route)  117 us
    pallas_call x1, Pallas kernels, factorize(): pl.pallas_call(factor_kernel, out_shape=(whole, whole), in_specs=[pl.Bloc...  50.1 us
    pallas_call x1, Pallas kernels, summed(): pl.pallas_call(functools.partial(reduce_kernel, n), out_shape=jax.ShapeDt...  32.5 us
    dot_general x1, matrix products, shards(): jnp.dot(left.reshape(MPOB * tall, bond), current, preferred_element_type=...  32.1 us
    pallas_call x1, Pallas kernels, mixed(): pl.pallas_call(functools.partial(mix_kernel, parts), grid=(own_rows // (2...  23.9 us
    dot_general x4, matrix products, shards(): jnp.dot(mixture, right[:, lanes], preferred_element_type=jnp.float32)  18.5 us
    ppermute x12, starting transfers between devices, sent(): return lax.ppermute(block, ('seg', 'bond'), route)  15.6 us
    unnamed x30, local copies, waits for them, and re-layouts  11.9 us
  transfers between devices with their start and end apart: 12, of which 4 were waited for; matrix products, arithmetic and copies ran while one was open for 25% of the time, Pallas kernels for 7%

profile of v1, /device:TPU:0, one launch (start us, length us, event | category | flops | bytes accessed | tf_op | source)
XLA Modules:
  0.0 360.2 jit_solution(10597398381495838909)
XLA Ops:
  1.2 2.7 collective-permute-start
  5.0 3.0 dynamic-slice_bitcast_fusion.6
  8.0 2.6 pad_maximum_fusion.9
  17.5 11.8 %collective-permute-done.6 = bf16[1024,1024]{1,0:T(8,128)(2,1)} collective-permute-done((bf16[1024,1024]{1,0:T(8,128)(2,1)}, bf16[1024,1024]{1,0:T(8,128)(2,1)}, u32[]{:S(2)}, u32[]{:S(2)}) %collective-permute-start.6) | collective-permute-done | bytes 2097184 | tf_op jit(solution)/shard_map/ppermute | solution.py:268
  29.2 2.9 collective-permute-start.4
  32.2 4.6 %fusion.24 = bf16[4,256,1024]{2,1,0:T(8,128)(2,1)S(1)} fusion(bf16[1024,1024]{1,0:T(8,128)(2,1)} %collective-permute-done.6, bf16[1024,4,256]{2,1,0:T(4,128)(2,1)} %bitcast.165), kind=kOutput, calls=%fused_computation.34 | convolution fusion | flops 2148532224 | bytes 6291456 | tf_op jit(solution)/shard_map/ab,bsc->sac/dot_general | solution.py:308
  41.4 2.5 copy.38
  47.1 72.6 %collective-permute-done.3 = bf16[256,2048]{1,0:T(8,128)(2,1)} collective-permute-done((bf16[256,2048]{1,0:T(8,128)(2,1)}, bf16[256,2048]{1,0:T(8,128)(2,1)}, u32[]{:S(2)}, u32[]{:S(2)}) %collective-permute-start.3) | collective-permute-done | bytes 1048608 | tf_op jit(solution)/shard_map/ppermute | solution.py:268
  125.9 2.7 pad_maximum_fusion.5
  128.6 2.8 copy.21
  131.4 3.0 fusion.45
  141.3 32.1 %fusion.projected_ref = f32[6,512,2048]{2,1,0:T(8,128)} fusion(bf16[6,256,1024]{2,1,0:T(8,128)(2,1)} %collective-permute-done.1, bf16[6,256,1024]{2,1,0:T(8,128)(2,1)} %collective-permute-done, bf16[1024,2048]{1,0:T(8,128)(2,1)S(1)} %copy-done.7), kind=kOutput, calls=%fused_computation | convolution fusion | flops 12897484800 | bytes 35651584 | tf_op jit(solution)/shard_map/dot_general | solution.py:319
  173.4 23.9 %mixed.1 = bf16[4,512,3072]{2,1,0:T(8,128)(2,1)S(1)} custom-call(bf16[192,192]{1,0:T(8,128)(2,1)S(1)} %mul.103.spread_ref, f32[6,512,2048]{2,1,0:T(8,128)} %fusion.projected_ref), custom_call_target="tpu_custom_call" | custom-call | flops 2415919104 | bytes 37748736 | tf_op jit(solution)/shard_map/mixed/pallas_call | solution.py:235
  197.3 6.0 %pad_maximum_fusion = bf16[12,256,1024]{2,1,0:T(8,128)(2,1)} fusion(bf16[6,256,1024]{2,1,0:T(8,128)(2,1)} %collective-permute-done.5, bf16[6,256,1024]{2,1,0:T(8,128)(2,1)} %bitcast.14), kind=kLoop, calls=%fused_computation.4 | loop fusion | flops 3145728 | bytes 12582912 | tf_op jit(solution)/shard_map/concatenate | solution.py:306
  203.3 6.1 %fusion.13 = f32[2048,256]{1,0:T(8,128)S(1)} fusion(f32[2048,256]{1,0:T(8,128)} %fusion.45, bf16[2048,3072]{1,0:T(8,128)(2,1)S(1)} %bitcast.118, bf16[3072,1024]{1,0:T(8,128)(2,1)} %bitcast.132), kind=kOutput, calls=%fused_computation.21 | convolution fusion | flops 3222274048 | bytes 18350080 | tf_op jit(solution)/shard_map/dot_general | solution.py:328
  211.1 4.0 %fusion.14 = f32[2048,256]{1,0:T(8,128)S(1)} fusion(f32[2048,256]{1,0:T(8,128)S(1)} %copy-done.3, bf16[2048,3072]{1,0:T(8,128)(2,1)S(1)} %bitcast.119, bf16[3072,1024]{1,0:T(8,128)(2,1)S(1)} %bitcast.133), kind=kOutput, calls=%fused_computation.22 | convolution fusion | flops 3222274048 | bytes 18350080 | tf_op jit(solution)/shard_map/dot_general | solution.py:328
  216.5 4.0 %fusion.16 = f32[2048,256]{1,0:T(8,128)S(1)} fusion(f32[2048,256]{1,0:T(8,128)S(1)} %copy-done.2, bf16[2048,3072]{1,0:T(8,128)(2,1)S(1)} %bitcast.120, bf16[3072,1024]{1,0:T(8,128)(2,1)S(1)} %bitcast.134), kind=kOutput, calls=%fused_computation.24 | convolution fusion | flops 3222274048 | bytes 18350080 | tf_op jit(solution)/shard_map/dot_general | solution.py:328
  222.1 4.4 %fusion.15 = f32[2048,256]{1,0:T(8,128)S(1)} fusion(f32[2048,256]{1,0:T(8,128)S(1)} %copy-done.1, bf16[2048,3072]{1,0:T(8,128)(2,1)S(1)} %bitcast.121, bf16[3072,1024]{1,0:T(8,128)(2,1)S(1)} %bitcast.135), kind=kOutput, calls=%fused_computation.23 | convolution fusion | flops 3222274048 | bytes 18350080 | tf_op jit(solution)/shard_map/dot_general | solution.py:328
  227.2 28.6 %collective-permute-done.11 = bf16[4,256,256]{2,1,0:T(8,128)(2,1)S(1)} collective-permute-done((bf16[4,256,256]{2,1,0:T(8,128)(2,1)S(1)}, bf16[4,256,256]{2,1,0:T(8,128)(2,1)S(1)}, u32[]{:S(2)}, u32[]{:S(2)}) %collective-permute-start.11) | collective-permute-done | bytes 524320 | tf_op jit(solution)/shard_map/ppermute | solution.py:268
  257.0 4.4 %collective-permute-done.10 = bf16[4,256,256]{2,1,0:T(8,128)(2,1)S(1)} collective-permute-done((bf16[4,256,256]{2,1,0:T(8,128)(2,1)S(1)}, bf16[4,256,256]{2,1,0:T(8,128)(2,1)S(1)}, u32[]{:S(2)}, u32[]{:S(2)}) %collective-permute-start.10) | collective-permute-done | bytes 524320 | tf_op jit(solution)/shard_map/ppermute | solution.py:268
  266.5 32.5 %summed.1 = f32[4,64,2560]{2,1,0:T(8,128)S(1)} custom-call(f32[4,64,2560]{2,1,0:T(8,128)S(1)} %bitcast.122), custom_call_target="tpu_custom_call" | custom-call | tf_op jit(solution)/shard_map/summed/pallas_call | solution.py:91
  299.0 50.1 %factorize.1 = (f32[1024,1024]{1,0:T(8,128)S(1)}, f32[1024,1024]{1,0:T(8,128)S(1)}) custom-call(f32[256,2560]{1,0:T(8,128)S(1)} %bitcast.123), custom_call_target="tpu_custom_call" | custom-call | tf_op jit(solution)/shard_map/factorize/pallas_call | solution.py:187
  349.0 7.0 %multiply_convert_fusion = bf16[1024,1024]{1,0:T(8,128)(2,1)S(1)} fusion(f32[1024,1024]{1,0:T(8,128)S(1)} %get-tuple-element.4, f32[1024,256]{1,0:T(8,128)S(1)} %bitcast.131, f32[1024,256]{1,0:T(8,128)S(1)} %bitcast.144, f32[1024,256]{1,0:T(8,128)S(1)} %bitcast.158, f32[1024,256]{1,0:T(8,128)S(1)} %bitcast.160), kind=kOutput, calls=%fused_computation.7 | convolution fusion | flops 6447693824 | bytes 10485760 | tf_op jit(solution)/shard_map/dot_general | solution.py:350
  356.0 2.9 copy.53
  (76 shorter events, 42.0 us)
Async XLA Ops:
  0.6 28.6 %collective-permute-start.6 = (bf16[1024,1024]{1,0:T(8,128)(2,1)}, bf16[1024,1024]{1,0:T(8,128)(2,1)}, u32[]{:S(2)}, u32[]{:S(2)}) collective-permute-start(bf16[1024,1024]{1,0:T(8,128)(2,1)} %bitcast.164), channel_id=1, source_target_pairs={{28,0},{29,1},{30,2},{31,3},{0,4},{1,5},{2,6},{3,7},{4,8},{5,9},{6... | collective-permute-start | bytes 6291464 | tf_op jit(solution)/shard_map/ppermute | solution.py:268
  1.2 139.2 %collective-permute-start = (bf16[6,256,1024]{2,1,0:T(8,128)(2,1)}, bf16[6,256,1024]{2,1,0:T(8,128)(2,1)}, u32[]{:S(2)}, u32[]{:S(2)}) collective-permute-start(bf16[6,256,1024]{2,1,0:T(8,128)(2,1)} %bitcast.162), channel_id=1, source_target_pairs={{28,0},{29,1},{30,2},{31,3},{0,4},{1,5},{2,6},{3,7},{4,8},{5,9},{6... | collective-permute-start | bytes 9437192 | tf_op jit(solution)/shard_map/ppermute | solution.py:268
  3.8 136.6 %collective-permute-start.1 = (bf16[6,256,1024]{2,1,0:T(8,128)(2,1)}, bf16[6,256,1024]{2,1,0:T(8,128)(2,1)}, u32[]{:S(2)}, u32[]{:S(2)}) collective-permute-start(bf16[6,256,1024]{2,1,0:T(8,128)(2,1)} %bitcast.163), channel_id=1, source_target_pairs={{30,0},{31,1},{28,2},{29,3},{2,4},{3,5},{0,6},{1,7},{6,8},{7,9},{4... | collective-permute-start | bytes 9437192 | tf_op jit(solution)/shard_map/ppermute | solution.py:268
  11.9 27.0 %collective-permute-start.2 = (bf16[256,2048]{1,0:T(8,128)(2,1)}, bf16[256,2048]{1,0:T(8,128)(2,1)S(1)}, u32[]{:S(2)}, u32[]{:S(2)}) collective-permute-start(bf16[256,2048]{1,0:T(8,128)(2,1)} %bitcast.61), channel_id=1, source_target_pairs={{1,0},{0,1},{3,2},{2,3},{5,4},{4,5},{7,6},{6,7},{9,8},{8,9},{11,10... | collective-permute-start | bytes 3145736 | tf_op jit(solution)/shard_map/ppermute | solution.py:268
  13.4 3.0 copy-start.12
  14.7 105.1 %collective-permute-start.3 = (bf16[256,2048]{1,0:T(8,128)(2,1)}, bf16[256,2048]{1,0:T(8,128)(2,1)}, u32[]{:S(2)}, u32[]{:S(2)}) collective-permute-start(bf16[256,2048]{1,0:T(8,128)(2,1)} %bitcast.63), channel_id=1, source_target_pairs={{2,0},{3,1},{0,2},{1,3},{6,4},{7,5},{4,6},{5,7},{10,8},{11,9},{8,1... | collective-permute-start | bytes 3145736 | tf_op jit(solution)/shard_map/ppermute | solution.py:268
  29.2 93.3 %collective-permute-start.4 = (bf16[256,2048]{1,0:T(8,128)(2,1)}, bf16[256,2048]{1,0:T(8,128)(2,1)}, u32[]{:S(2)}, u32[]{:S(2)}) collective-permute-start(bf16[256,2048]{1,0:T(8,128)(2,1)} %bitcast.155), channel_id=1, source_target_pairs={{3,0},{2,1},{1,2},{0,3},{7,4},{6,5},{5,6},{4,7},{11,8},{10,9},{9,1... | collective-permute-start | bytes 3145736 | tf_op jit(solution)/shard_map/ppermute | solution.py:268
  37.9 2.6 copy-start.11
  39.9 84.0 %collective-permute-start.7 = (bf16[4,512,256]{1,2,0:T(8,128)(2,1)}, bf16[4,512,256]{1,2,0:T(8,128)(2,1)}, u32[]{:S(2)}, u32[]{:S(2)}) collective-permute-start(bf16[4,512,256]{1,2,0:T(8,128)(2,1)} %pad_maximum_fusion.12), channel_id=1, source_target_pairs={{1,0},{0,1},{3,2},{2,3},{5,4},{4,5},{7,6},{6,7},{9,8},{8,9},{11,10... | collective-permute-start | bytes 3145736 | tf_op jit(solution)/shard_map/ppermute | solution.py:268
  44.6 1.2 copy-start.5
  45.8 1.2 copy-start.10
  119.8 6.1 %copy-start.8 = (bf16[4,256,256]{1,2,0:T(8,128)(2,1)S(1)}, bf16[4,256,256]{1,2,0:T(8,128)(2,1)}, u32[]{:S(2)}) copy-start(bf16[4,256,256]{1,2,0:T(8,128)(2,1)} %get-tuple-element.17) | copy-start | bytes 1572868
  119.8 77.5 %collective-permute-start.5 = (bf16[6,256,1024]{2,1,0:T(8,128)(2,1)}, bf16[6,256,1024]{2,1,0:T(8,128)(2,1)}, u32[]{:S(2)}, u32[]{:S(2)}) collective-permute-start(bf16[6,256,1024]{2,1,0:T(8,128)(2,1)} %bitcast.14), channel_id=1, source_target_pairs={{1,0},{0,1},{3,2},{2,3},{5,4},{4,5},{7,6},{6,7},{9,8},{8,9},{11,10... | collective-permute-start | bytes 9437192 | tf_op jit(solution)/shard_map/ppermute | solution.py:268
  123.9 2.0 copy-start.6
  131.4 3.0 copy-start
  138.4 2.9 copy-start.7
  203.3 7.8 %copy-start.3 = (f32[2048,256]{1,0:T(8,128)S(1)}, f32[2048,256]{1,0:T(8,128)}, u32[]{:S(2)}) copy-start(f32[2048,256]{1,0:T(8,128)} %fusion.48) | copy-start | bytes 6291460
  203.3 7.8 %copy-start.4 = (bf16[12,256,1024]{2,1,0:T(8,128)(2,1)S(1)}, bf16[12,256,1024]{2,1,0:T(8,128)(2,1)}, u32[]{:S(2)}) copy-start(bf16[12,256,1024]{2,1,0:T(8,128)(2,1)} %pad_maximum_fusion) | copy-start | bytes 18874372
  209.5 7.0 %copy-start.2 = (f32[2048,256]{1,0:T(8,128)S(1)}, f32[2048,256]{1,0:T(8,128)}, u32[]{:S(2)}) copy-start(f32[2048,256]{1,0:T(8,128)} %fusion.50) | copy-start | bytes 6291460
  209.5 54.6 %collective-permute-start.8 = (bf16[4,256,256]{2,1,0:T(8,128)(2,1)S(1)}, bf16[4,256,256]{2,1,0:T(8,128)(2,1)S(1)}, u32[]{:S(2)}, u32[]{:S(2)}) collective-permute-start(bf16[4,256,256]{2,1,0:T(8,128)(2,1)S(1)} %fusion.37), channel_id=1, source_target_pairs={{2,0},{3,1},{0,2},{1,3},{6,4},{7,5},{4,6},{5,7},{10,8},{11,9},{8,1... | collective-permute-start | bytes 1572872 | tf_op jit(solution)/shard_map/ppermute | solution.py:268
  216.0 6.2 %copy-start.1 = (f32[2048,256]{1,0:T(8,128)S(1)}, f32[2048,256]{1,0:T(8,128)}, u32[]{:S(2)}) copy-start(f32[2048,256]{1,0:T(8,128)} %fusion.42) | copy-start | bytes 6291460
  216.0 40.9 %collective-permute-start.9 = (bf16[4,256,256]{2,1,0:T(8,128)(2,1)}, bf16[4,256,256]{2,1,0:T(8,128)(2,1)S(1)}, u32[]{:S(2)}, u32[]{:S(2)}) collective-permute-start(bf16[4,256,256]{2,1,0:T(8,128)(2,1)} %fusion.38), channel_id=1, source_target_pairs={{2,0},{3,1},{0,2},{1,3},{6,4},{7,5},{4,6},{5,7},{10,8},{11,9},{8,1... | collective-permute-start | bytes 1572872 | tf_op jit(solution)/shard_map/ppermute | solution.py:268
  220.5 35.2 %collective-permute-start.11 = (bf16[4,256,256]{2,1,0:T(8,128)(2,1)S(1)}, bf16[4,256,256]{2,1,0:T(8,128)(2,1)S(1)}, u32[]{:S(2)}, u32[]{:S(2)}) collective-permute-start(bf16[4,256,256]{2,1,0:T(8,128)(2,1)S(1)} %fusion.40), channel_id=1, source_target_pairs={{2,0},{3,1},{0,2},{1,3},{6,4},{7,5},{4,6},{5,7},{10,8},{11,9},{8,1... | collective-permute-start | bytes 1572872 | tf_op jit(solution)/shard_map/ppermute | solution.py:268
  226.6 34.8 %collective-permute-start.10 = (bf16[4,256,256]{2,1,0:T(8,128)(2,1)S(1)}, bf16[4,256,256]{2,1,0:T(8,128)(2,1)S(1)}, u32[]{:S(2)}, u32[]{:S(2)}) collective-permute-start(bf16[4,256,256]{2,1,0:T(8,128)(2,1)S(1)} %fusion.39), channel_id=1, source_target_pairs={{2,0},{3,1},{0,2},{1,3},{6,4},{7,5},{4,6},{5,7},{10,8},{11,9},{8,1... | collective-permute-start | bytes 1572872 | tf_op jit(solution)/shard_map/ppermute | solution.py:268
  (1 other events, 1.0 us)

commit v2 on v0

--- a/solution.py
+++ b/solution.py
@@ -15,12 +15,8 @@
 GROUP = 4
 ROWS = 8
 WAVES = 2
-
-
-def shifted(block, axis, distance):
-    devices = range(lax.axis_size(axis))
-    route = [((i - distance) % len(devices), i) for i in devices]
-    return lax.ppermute(block, axis, route)
+EDGES = 4
+LEFT_ROWS = 64
 
 
 def halves(x):
@@ -204,96 +200,371 @@
     )(packed)
 
 
-def mix_kernel(parts, spread_ref, projected_ref, mixture_ref):
-    width = projected_ref.shape[2] // PHYS
-    spread = spread_ref[...]
-    results = []
-    for first in range(0, 2 * ROWS, ROWS):
-        stack = jnp.concatenate(
-            [
-                projected_ref[u, first : first + ROWS, t * width : (t + 1) * width]
-                for u in range(MPOB)
-                for t in range(PHYS)
-            ],
-            axis=0,
+def minor_size(n):
+    return max(d for d in range(1, n + 1) if n % d == 0 and d * d <= n)
+
+
+def edge_spans(width):
+    unit = width // EDGES
+    return [(j * unit, unit) for j in range(EDGES)]
+
+
+def front_kernel(
+    segments, n, left_ref, prev_left_ref, current_ref, right_ref,
+    prev_site_ref, prev_right_ref, spread_ref, target_ref,
+    left, current, right, prev_left, partial_out, partial_in, projected, mixture, outgoing, incoming,
+    left_send, left_recv, prev_send, prev_recv, major_send, major_recv, minor_send, minor_recv,
+    relay_send, relay_recv, right_send, right_recv, partial_send, partial_recv,
+    target_send, target_recv, local_sem,
+):
+    q = minor_size(n)
+    p = n // q
+    seg, index = lax.axis_index("seg"), lax.axis_index("bond")
+    major, minor = index // q, lax.rem(index, q)
+    own, bond = left_ref.shape[1], left_ref.shape[2]
+    wide, tall = q * own, p * own
+    half = own // 2
+    rows = projected.shape[1] // MPOB
+    chunks = own // rows
+    spans = edge_spans(bond)
+
+    def device(hop, dm, dr):
+        m, r = lax.rem(major + dm, p), lax.rem(minor + dr, q)
+        return {"seg": lax.rem(seg + hop, segments), "bond": m * q + r}
+
+    def copy(src, dst, send, recv, to):
+        return pltpu.make_async_remote_copy(
+            src_ref=src, dst_ref=dst, send_sem=send, recv_sem=recv, device_id=to
         )
-        high, low = halves(stack)
-        results.append(
-            jnp.dot(spread, high, preferred_element_type=jnp.float32)
-            + jnp.dot(spread, low, preferred_element_type=jnp.float32)
+
+    def slot(d):
+        return lax.rem(major + d, p)
+
+    def place(dm, dr):
+        return (lax.rem(major + dm, p) * q + lax.rem(minor + dr, q)) * own
+
+    barrier = pltpu.get_barrier_semaphore()
+    peers = [device(0, d, 0) for d in range(1, p)] + [device(0, 0, d) for d in range(1, q)]
+    peers += [device(hop, d, 0) for d in range(p) for hop in (1, segments - 1)]
+    for peer in peers:
+        pl.semaphore_signal(barrier, inc=1, device_id=peer)
+    pl.semaphore_wait(barrier, len(peers))
+
+    def left_flow(d, j, slot_index, back):
+        span = pl.ds(pl.multiple_of(j * rows, rows), rows)
+        return copy(
+            left_ref.at[:, span, :],
+            left.at[slot_index, :, span, :],
+            left_send.at[d, j],
+            left_recv.at[back, j],
+            device(1, d, 0),
         )
-    for v in range(MPOB):
-        for s in range(PHYS):
-            at = (v * PHYS + s) * ROWS
-            both = jnp.concatenate([one[at : at + ROWS, :] for one in results], axis=0)
-            both = both.astype(jnp.bfloat16)
-            part = width // parts
-            for p in range(parts):
-                start = (p * MPOB + v) * part
-                mixture_ref[s, :, start : start + part] = both[:, p * part : (p + 1) * part]
-
-
-def mixed(projected, coupling, parts):
-    own_rows, width = projected.shape[1], projected.shape[2] // PHYS
+
+    def left_out(d, j):
+        return left_flow(d, j, major, (p - d) % p)
+
+    def left_in(d, j):
+        return left_flow(d, j, slot(d), d)
+
+    def current_rows(dm, dr, h):
+        return pl.ds(pl.multiple_of(place(dm, dr) + h * half, half), half)
+
+    def source_columns(dm):
+        return pl.ds(pl.multiple_of(slot(dm) * wide, wide), wide)
+
+    prev_flow = copy(prev_left_ref, prev_left, prev_send.at[0], prev_recv.at[0], device(1, 0, 0))
+    prev_flow.start()
+    sends = [prev_flow]
+    for h in range(2):
+        source = pl.ds(h * half, half)
+        for d in range(1, p):
+            flow = copy(
+                current_ref.at[:, source, source_columns(d)],
+                current.at[:, current_rows(0, 0, h), :],
+                major_send.at[d, h],
+                major_recv.at[p - d, h],
+                device(0, d, 0),
+            )
+            flow.start()
+            sends.append(flow)
+        for d in range(1, q):
+            flow = copy(
+                current_ref.at[:, source, source_columns(0)],
+                current.at[:, current_rows(0, 0, h), :],
+                minor_send.at[d, h],
+                minor_recv.at[q - d, h],
+                device(0, 0, d),
+            )
+            flow.start()
+            sends.append(flow)
+    for j in range(chunks):
+        for d in range(p):
+            flow = left_out(d, j)
+            flow.start()
+            sends.append(flow)
+    locals_ = [
+        pltpu.make_async_copy(
+            current_ref.at[:, :, source_columns(0)],
+            current.at[:, pl.ds(pl.multiple_of(place(0, 0), own), own), :],
+            local_sem.at[0],
+        ),
+        pltpu.make_async_copy(
+            right_ref, right.at[:, pl.ds(pl.multiple_of(minor * own, own), own), :], local_sem.at[1]
+        ),
+    ]
+    for one in locals_:
+        one.start()
+
+    for h in range(2):
+        for dm in range(1, p):
+            landed = current.at[:, current_rows(dm, 0, h), :]
+            copy(
+                landed, landed, major_send.at[dm, h], major_recv.at[dm, h], device(0, dm, 0)
+            ).wait_recv()
+            for d in range(1, q):
+                flow = copy(
+                    landed, landed, relay_send.at[dm, d, h], relay_recv.at[dm, q - d, h],
+                    device(0, 0, d),
+                )
+                flow.start()
+                sends.append(flow)
+
+    prev_flow.wait_recv()
+
+    def contract(d, out):
+        def body(step, carry):
+            m, s = step // PHYS, lax.rem(step, PHYS)
+            top = (m * q + lax.rem(minor + d, q)) * own
+            value = jnp.dot(
+                prev_left[pl.ds(pl.multiple_of(top, own), own), :],
+                prev_site_ref[s],
+                preferred_element_type=jnp.float32,
+            )
+            out[s, pl.ds(pl.multiple_of(m * own, own), own), :] = value.astype(jnp.bfloat16)
+            return carry
+
+        lax.fori_loop(0, p * PHYS, body, 0)
+
+    for d in range(1, q):
+        contract(d, partial_out.at[d - 1])
+        flow = copy(
+            partial_out.at[d - 1], partial_in.at[minor], partial_send.at[d],
+            partial_recv.at[q - d], device(0, 0, d),
+        )
+        flow.start()
+        sends.append(flow)
+
+    def right_flow(d, j, row, back):
+        first, width = spans[j]
+        lanes = pl.ds(first, width)
+        return copy(
+            right_ref.at[:, :, lanes],
+            right.at[:, pl.ds(pl.multiple_of(row * own, own), own), lanes],
+            right_send.at[d, j],
+            right_recv.at[back, j],
+            device(0, 0, d),
+        )
+
+    for j in range(len(spans)):
+        for d in range(1, q):
+            flow = right_flow(d, j, minor, q - d)
+            flow.start()
+            sends.append(flow)
+    contract(0, partial_in.at[minor])
+
+    for h in range(2):
+        for d in range(1, q):
+            landed = current.at[:, current_rows(0, d, h), :]
+            copy(
+                landed, landed, minor_send.at[d, h], minor_recv.at[d, h], device(0, 0, d)
+            ).wait_recv()
+            for dm in range(1, p):
+                landed = current.at[:, current_rows(dm, d, h), :]
+                copy(
+                    landed, landed, relay_send.at[dm, d, h], relay_recv.at[dm, d, h],
+                    device(0, 0, d),
+                ).wait_recv()
+    for one in locals_:
+        one.wait()
+
+    def mix(step, carry):
+        j, order = step // p, lax.rem(step, p)
+        where = lax.rem(major + order, p)
+        left_in(order, j).wait_recv()
+        span = pl.ds(pl.multiple_of(j * rows, rows), rows)
+        block = left[where, :, span, :].reshape(MPOB * rows, bond)
+
+        def project(t, carry):
+            projected[t] = jnp.dot(block, current[t], preferred_element_type=jnp.float32)
+            return carry
+
+        lax.fori_loop(0, PHYS, project, 0)
+
+        def spread(g, carry):
+            results = []
+            for first in range(2):
+                at = g * 2 * ROWS + first * ROWS
+                stack = jnp.concatenate(
+                    [
+                        projected[t, pl.ds(pl.multiple_of(u * rows + at, ROWS), ROWS), :]
+                        for u in range(MPOB)
+                        for t in range(PHYS)
+                    ],
+                    axis=0,
+                )
+                results.append(
+                    jnp.dot(
+                        spread_ref[...],
+                        stack.astype(jnp.bfloat16),
+                        preferred_element_type=jnp.float32,
+                    )
+                )
+            top = pl.multiple_of(where * own + j * rows + g * 2 * ROWS, 2 * ROWS)
+            for v in range(MPOB):
+                for s in range(PHYS):
+                    first = (v * PHYS + s) * ROWS
+                    both = jnp.concatenate([one[first : first + ROWS] for one in results], axis=0)
+                    mixture[s, pl.ds(top, 2 * ROWS), v * wide : (v + 1) * wide] = both.astype(
+                        jnp.bfloat16
+                    )
+            return carry
+
+        lax.fori_loop(0, rows // (2 * ROWS), spread, 0)
+        return carry
+
+    lax.fori_loop(0, chunks * p, mix, 0)
+
+    for d in range(1, q):
+        landed = partial_in.at[lax.rem(minor + d, q)]
+        copy(
+            landed, landed, partial_send.at[d], partial_recv.at[d], device(0, 0, d)
+        ).wait_recv()
+
+    def products(d, j, write):
+        first, width = spans[j]
+
+        def body(s, carry):
+            top = pl.ds(pl.multiple_of(slot(d) * own, own), own)
+            lanes = slice(first, first + width)
+            value = 2.0 * jnp.dot(
+                mixture[s, top, :],
+                right[:, :, lanes].reshape(MPOB * wide, width),
+                preferred_element_type=jnp.float32,
+            )
+            for r in range(q):
+                prev_rows = pl.ds(pl.multiple_of(major * wide + r * own, own), own)
+                value = value - jnp.dot(
+                    partial_in[r, s, top, :],
+                    prev_right_ref[prev_rows, lanes],
+                    preferred_element_type=jnp.float32,
+                )
+            write(s, lanes, value)
+            return carry
+
+        lax.fori_loop(0, PHYS, body, 0)
+
+    def target_flow(d, j, back):
+        first, width = spans[j]
+        lanes = pl.ds(first, width)
+        return copy(
+            outgoing.at[d - 1, :, :, lanes], incoming.at[back - 1, :, :, lanes],
+            target_send.at[d, j], target_recv.at[back, j], device(0, d, 0),
+        )
+
+    for j in range(len(spans)):
+        for d in range(1, q):
+            right_flow(d, j, lax.rem(minor + d, q), d).wait_recv()
+        for d in range(1, p):
+
+            def keep(s, lanes, value):
+                outgoing[d - 1, s, :, lanes] = value.astype(jnp.bfloat16)
+
+            products(d, j, keep)
+            flow = target_flow(d, j, p - d)
+            flow.start()
+            sends.append(flow)
+
+        def own_part(s, lanes, value):
+            target_ref[s, :, lanes] = value
+
+        products(0, j, own_part)
+    for j, (first, width) in enumerate(spans):
+        for d in range(1, p):
+            target_flow(d, j, d).wait_recv()
+            lanes = slice(first, first + width)
+
+            def add(s, carry):
+                target_ref[s, :, lanes] += incoming[d - 1, s, :, lanes].astype(jnp.float32)
+                return carry
+
+            lax.fori_loop(0, PHYS, add, 0)
+    for flow in sends:
+        flow.wait_send()
+
+
+def front(left, prev_left, current, right, prev_site, prev_right, coupling):
+    n, segments = lax.axis_size("bond"), lax.axis_size("seg")
+    q = minor_size(n)
+    p = n // q
+    own, bond = left.shape[1], left.shape[2]
+    wide, tall = q * own, p * own
+    rows = min(LEFT_ROWS, own)
+    edges = len(edge_spans(bond))
     side = MPOB * PHYS * ROWS
     diagonal = jnp.eye(ROWS, dtype=coupling.dtype)
     turned = jnp.transpose(coupling, (1, 2, 0, 3))
     spread = turned[:, :, None, :, :, None] * diagonal[None, None, :, None, None, :]
+    low, full = jnp.bfloat16, jnp.float32
+    whole = pl.BlockSpec(memory_space=pltpu.VMEM)
+    there = pl.BlockSpec(memory_space=pl.ANY)
+
+    def pairs(*shape):
+        return [pltpu.SemaphoreType.DMA(shape)] * 2
+
     return pl.pallas_call(
-        functools.partial(mix_kernel, parts),
-        grid=(own_rows // (2 * ROWS),),
-        out_shape=jax.ShapeDtypeStruct((PHYS, own_rows, MPOB * width), jnp.bfloat16),
-        in_specs=[
-            pl.BlockSpec((side, side), lambda i: (0, 0)),
-            pl.BlockSpec((MPOB, 2 * ROWS, PHYS * width), lambda i: (0, i, 0)),
-        ],
-        out_specs=pl.BlockSpec((PHYS, 2 * ROWS, MPOB * width), lambda i: (0, i, 0)),
-        compiler_params=pltpu.CompilerParams(vmem_limit_bytes=40 * 2**20),
-        cost_estimate=pl.CostEstimate(
-            flops=4 * side * MPOB * PHYS * own_rows * width,
-            bytes_accessed=6 * MPOB * PHYS * own_rows * width,
-            transcendentals=0,
+        functools.partial(front_kernel, segments, n),
+        out_shape=jax.ShapeDtypeStruct((PHYS, own, bond), full),
+        in_specs=[there] * 4 + [whole] * 3,
+        out_specs=whole,
+        scratch_shapes=[
+            pltpu.VMEM((p, MPOB, own, bond), low),
+            pltpu.VMEM((PHYS, bond, wide), low),
+            pltpu.VMEM((MPOB, wide, bond), low),
+            pltpu.VMEM((bond, bond), low),
+            pltpu.VMEM((max(q - 1, 1), PHYS, tall, own), low),
+            pltpu.VMEM((q, PHYS, tall, own), low),
+            pltpu.VMEM((PHYS, MPOB * rows, wide), full),
+            pltpu.VMEM((PHYS, tall, MPOB * wide), low),
+            pltpu.VMEM((max(p - 1, 1), PHYS, own, bond), low),
+            pltpu.VMEM((max(p - 1, 1), PHYS, own, bond), low),
+        ]
+        + pairs(p, own // rows)
+        + pairs(1)
+        + pairs(p, 2)
+        + pairs(q, 2)
+        + pairs(p, q, 2)
+        + pairs(q, edges)
+        + pairs(q)
+        + pairs(p, edges)
+        + [pltpu.SemaphoreType.DMA((2,))],
+        compiler_params=pltpu.CompilerParams(
+            collective_id=1, has_side_effects=True, vmem_limit_bytes=56 * 2**20
         ),
-        name="mixed",
-    )(spread.reshape(side, side), projected)
+        name="front",
+    )(left, prev_left, current, right, prev_site, prev_right, spread.reshape(side, side))
 
 
 def shards(left_env, prev_left, cur_site, prev_site, hamiltonian, right_env, prev_right):
-    left_now, prev_now = shifted((left_env[0], prev_left[0]), "seg", 1)
-    own_rows = left_now.shape[0]
-    bond_width = left_now.shape[2]
-    current = lax.all_gather(cur_site[0], "bond", axis=0, tiled=True)
-    left_terms = jnp.transpose(left_now, (1, 0, 2)).reshape(MPOB * own_rows, bond_width)
-    projected = jnp.dot(
-        left_terms,
-        current.reshape(bond_width, PHYS * bond_width),
-        preferred_element_type=jnp.float32,
-    ).reshape(MPOB, own_rows, PHYS * bond_width)
-    parts = lax.axis_size("bond") if own_rows % 128 == 0 else 1
-    mixture = mixed(projected, hamiltonian[0], parts)
-    partial_value = jnp.einsum(
-        "ab,bsc->asc", prev_now, prev_site[0], preferred_element_type=jnp.float32
-    ).astype(jnp.bfloat16)
-    second = jnp.einsum(
-        "akc,cy->kay",
-        lax.all_to_all(partial_value, "bond", split_axis=0, concat_axis=2, tiled=True),
+    own_rows, bond_width = left_env.shape[1], left_env.shape[3]
+    target = front(
+        jnp.transpose(left_env[0], (1, 0, 2)),
+        prev_left[0],
+        jnp.transpose(cur_site[0], (1, 0, 2)),
+        jnp.transpose(right_env[0], (1, 0, 2)),
+        jnp.transpose(prev_site[0], (1, 0, 2)),
         prev_right[0],
-        preferred_element_type=jnp.float32,
-    )
-    flat_rows = own_rows * PHYS
-    right_terms = jnp.transpose(right_env[0], (1, 0, 2))
-    if parts > 1:
-        right = lax.all_gather(
-            right_terms.reshape(MPOB * own_rows, bond_width), "bond", axis=0, tiled=True
-        )
-    else:
-        right = lax.all_gather(right_terms, "bond", axis=1, tiled=True)
-    applied = jnp.dot(
-        mixture.reshape(flat_rows, MPOB * bond_width),
-        right.reshape(MPOB * bond_width, bond_width),
-        preferred_element_type=jnp.float32,
-    )
-    target = 2.0 * applied - second.reshape(flat_rows, bond_width)
+        hamiltonian[0],
+    ).reshape(PHYS * own_rows, bond_width)
     strips = [
         jnp.dot(
             target[:, start : start + STRIP].T,

time: 393 us -> 306 us (0.78)
  waiting for transfers between devices: 142 us -> 0 us
  Pallas kernels: 128 us -> 268 us
  matrix products: 61.7 us -> 18.3 us
  local copies, waits for them, and re-layouts: 36.6 us -> 13.9 us
  between operations: 14.2 us -> 0.76 us
  starting transfers between devices: 8.05 us -> 0 us
    pallas_call x1, Pallas kernels: 17.9 us -> 160 us  [front(): pl.pallas_call(functools.partial(front_kernel, segments, n), out_shape=ja...]
    all_gather x2 -> x0, waiting for transfers between devices: 83.5 us -> none  [the longest x1 63.9 us: shards(): lax.all_gather(right_terms.reshape(MPOB * own_rows, bond_width), 'bond',...]
    dot_general x4 -> x0, matrix products: 49.1 us -> none  [the longest x1 21.2 us: shards(): jnp.dot(left_terms, current.reshape(bond_width, PHYS * bond_width), prefe...]
    all_to_all x1 -> x0, waiting for transfers between devices: 31.6 us -> none  [shards(): lax.all_to_all(partial_value, 'bond', split_axis=0, concat_axis=2, tiled=...]
    ppermute x2 -> x0, waiting for transfers between devices: 25.3 us -> none  [shifted(): return lax.ppermute(block, axis, route)]
    reshape x1 -> x0, local copies, waits for them, and re-layouts: 14.7 us -> none  [shards(): current.reshape(bond_width, PHYS * bond_width)]
    all_to_all x2 -> x0, local copies, waits for them, and re-layouts: 8.96 us -> none  [shards(): lax.all_to_all(partial_value, 'bond', split_axis=0, concat_axis=2, tiled=...]
    all_to_all x1 -> x0, starting transfers between devices: 4.76 us -> none  [shards(): lax.all_to_all(partial_value, 'bond', split_axis=0, concat_axis=2, tiled=...]
  transfers between devices with their start and end apart: 5 -> 0, of which waited for: 4 -> 0; matrix products, arithmetic and copies ran while one was open for 14% -> 0% of each run, Pallas kernels for 5% -> 0%
where the time goes in v2:
time: 306 us; the launch traced here: 304 us
  Pallas kernels  268 us (88%)
  matrix products  18.3 us (6%)
  local copies, waits for them, and re-layouts  13.9 us (5%)
  other arithmetic  3.22 us (1%)
    pallas_call x1, Pallas kernels, front(): pl.pallas_call(functools.partial(front_kernel, segments, n), out_shape=ja...  160 us
    pallas_call x1, Pallas kernels, summed(): pl.pallas_call(functools.partial(reduce_kernel, n), out_shape=jax.ShapeDt...  57.6 us
    pallas_call x1, Pallas kernels, factorize(): pl.pallas_call(factor_kernel, out_shape=(whole, whole), in_specs=[pl.Bloc...  49.9 us
    dot_general x1, matrix products, shards(): lax.dot_general(target, inverse, (((1,), (1,)), ((), ())), precision=lax....  9.8 us
    unnamed x12, local copies, waits for them, and re-layouts  9.21 us
    dot_general x4, matrix products, shards(): jnp.dot(target[:, start:start + STRIP].T, target[:, start:], precision=la...  8.54 us

profile of v2, /device:TPU:0, one launch (start us, length us, event | category | flops | bytes accessed | tf_op | source)
XLA Modules:
  0.0 303.9 jit_solution(1853884252031629945)
XLA Ops:
  0.6 0.0 copy-start.3
  0.6 3.3 %copy.19 = bf16[1,1024,4,256]{3,1,2,0:T(8,128)(2,1)} copy(bf16[1,1024,4,256]{3,2,1,0:T(4,128)(2,1)} %param.10) | data formatting | bytes 4194304 | tf_op args[3]
  4.0 0.0 copy-done.3
  4.0 1.9 copy.20
  5.9 0.0 copy-done.4
  5.9 0.4 copy.11
  6.3 0.6 broadcast_multiply_fusion
  7.0 1.4 mul.29.spread_ref
  8.3 160.1 %front.1 = f32[4,256,1024]{2,1,0:T(8,128)} custom-call(bf16[6,256,1024]{2,1,0:T(8,128)(2,1)} %bitcast.44, bf16[1024,1024]{1,0:T(8,128)(2,1)} %bitcast.46, bf16[4,256,1024]{2,1,0:T(8,128)(2,1)} %bitcast.43, bf16[6,256,1024]{2,1,0:T(8,128)(2,1)} %bitcast.45, bf16[4,1024,256]{2,1,0:T(8,128)(2,1)} %bitcast.42, bf16[1024,1024]{1,0:T(8,128)(2,1)} %bitcast.47, ...), custom_call_target="tpu_custom_call" | custom-call | tf_op jit(solution)/shard_map/front/pallas_call | solution.py:524
  168.5 0.0 copy-start.2
  168.5 4.6 %fusion.8 = f32[256,1024]{1,0:T(8,128)S(1)} fusion(f32[1024,1024]{1,0:T(8,128)} %bitcast.37), kind=kOutput, calls=%fused_computation.13 | convolution fusion | flops 1610612736 | bytes 6291456 | tf_op jit(solution)/shard_map/dot_general | solution.py:569
  173.1 0.0 copy-done.2
  173.1 1.8 fusion
  174.9 1.1 fusion.2
  176.0 1.0 fusion.4
  177.1 0.3 pad_maximum_fusion
  177.4 57.6 %summed.1 = f32[4,64,2560]{2,1,0:T(8,128)S(1)} custom-call(f32[4,64,2560]{2,1,0:T(8,128)S(1)} %bitcast.35), custom_call_target="tpu_custom_call" | custom-call | tf_op jit(solution)/shard_map/summed/pallas_call | solution.py:92
  234.9 49.9 %factorize.1 = (f32[1024,1024]{1,0:T(8,128)S(1)}, f32[1024,1024]{1,0:T(8,128)S(1)}) custom-call(f32[256,2560]{1,0:T(8,128)S(1)} %bitcast.36), custom_call_target="tpu_custom_call" | custom-call | tf_op jit(solution)/shard_map/factorize/pallas_call | solution.py:188
  284.9 0.0 copy-start
  284.9 1.9 copy-done
  286.8 2.0 copy-done.1
  288.8 2.3 multiply_bitcast_fusion
  291.1 9.8 %multiply_convert_fusion = bf16[1024,1024]{1,0:T(8,128)(2,1)S(1)} fusion(f32[1024,1024]{1,0:T(8,128)} %bitcast.38, f32[1024,1024]{1,0:T(8,128)} %copy-done.1), kind=kOutput, calls=%fused_computation | convolution fusion | flops 6444548096 | bytes 10485760 | tf_op jit(solution)/shard_map/dot_general | solution.py:580
  300.9 2.9 copy.18
  (3 shorter events, 0.0 us)
Async XLA Ops:
  0.6 3.3 %copy-start.3 = (bf16[1,256,4,1024]{3,2,1,0:T(4,128)(2,1)S(1)}, bf16[1,256,4,1024]{3,2,1,0:T(4,128)(2,1)}, u32[]{:S(2)}) copy-start(bf16[1,256,4,1024]{3,2,1,0:T(4,128)(2,1)} %param.9) | copy-start | bytes 6291460
  4.0 2.0 copy-start.4
  168.5 4.6 %copy-start.2 = (f32[4,256,1024]{2,1,0:T(8,128)S(1)}, f32[4,256,1024]{2,1,0:T(8,128)}, u32[]{:S(2)}) copy-start(f32[4,256,1024]{2,1,0:T(8,128)} %front.1) | copy-start | bytes 12582916
  284.9 2.0 copy-start
  286.8 2.0 copy-start.1

commit v3 on v2

--- a/solution.py
+++ b/solution.py
@@ -14,7 +14,7 @@
 STRIP = 256
 GROUP = 4
 ROWS = 8
-WAVES = 2
+AHEAD = 2
 EDGES = 4
 LEFT_ROWS = 64
 
@@ -24,86 +24,11 @@
     return high, (x - high.astype(jnp.float32)).astype(jnp.bfloat16)
 
 
-def product(a, b, dims):
-    a_high, a_low = halves(a)
-    b_high, b_low = halves(b)
-
+def split_dot(a, b, dims):
     def dot(x, y):
         return lax.dot_general(x, y, (dims, ((), ())), preferred_element_type=jnp.float32)
 
-    return dot(a_high, b_high) + (dot(a_high, b_low) + dot(a_low, b_high))
-
-
-def reduce_kernel(n, own_ref, out_ref, parts, total, send_sem, recv_sem, send_back, recv_back):
-    me = lax.axis_index("bond")
-    barrier = pltpu.get_barrier_semaphore()
-    peers = [lax.rem(me + d, n) for d in range(1, n)]
-    for peer in peers:
-        pl.semaphore_signal(barrier, inc=1, device_id={"bond": peer})
-    pl.semaphore_wait(barrier, n - 1)
-    width = own_ref.shape[2] // WAVES
-    waves = [pl.ds(w * width, width) for w in range(WAVES)]
-    outward, back = [], []
-    for w, lanes in enumerate(waves):
-        outward.append([
-            pltpu.make_async_remote_copy(
-                src_ref=own_ref.at[peer, :, lanes],
-                dst_ref=parts.at[d, :, lanes],
-                send_sem=send_sem.at[w, d],
-                recv_sem=recv_sem.at[w, d],
-                device_id={"bond": peer},
-            )
-            for d, peer in enumerate(peers)
-        ])
-        for copy in outward[w]:
-            copy.start()
-    for w, lanes in enumerate(waves):
-        for copy in outward[w]:
-            copy.wait_recv()
-        value = own_ref[me, :, lanes]
-        for d in range(n - 1):
-            value = value + parts[d, :, lanes]
-        total[me, :, lanes] = value
-        back.append([
-            pltpu.make_async_remote_copy(
-                src_ref=total.at[me, :, lanes],
-                dst_ref=total.at[me, :, lanes],
-                send_sem=send_back.at[w, d],
-                recv_sem=recv_back.at[w, d],
-                device_id={"bond": peer},
-            )
-            for d, peer in enumerate(peers)
-        ])
-        for copy in back[w]:
-            copy.start()
-    for w, lanes in enumerate(waves):
-        for copy in back[w]:
-            copy.wait_recv()
-        out_ref[:, :, lanes] = total[:, :, lanes]
-    for copies in outward + back:
-        for copy in copies:
-            copy.wait_send()
-
-
-def summed(packed):
-    n = lax.axis_size("bond")
-    rows, width = packed.shape
-    shape = (n, rows // n, width)
-    return pl.pallas_call(
-        functools.partial(reduce_kernel, n),
-        out_shape=jax.ShapeDtypeStruct(shape, jnp.float32),
-        in_specs=[pl.BlockSpec(memory_space=pltpu.VMEM)],
-        out_specs=pl.BlockSpec(memory_space=pltpu.VMEM),
-        scratch_shapes=[
-            pltpu.VMEM((n - 1,) + shape[1:], jnp.float32),
-            pltpu.VMEM(shape, jnp.float32),
-        ]
-        + [pltpu.SemaphoreType.DMA((WAVES, n - 1))] * 4,
-        compiler_params=pltpu.CompilerParams(
-            collective_id=0, has_side_effects=True, vmem_limit_bytes=24 * 2**20
-        ),
-        name="summed",
-    )(packed.reshape(shape)).reshape(rows, width)
+    return dot(a[0], b[0]) + (dot(a[0], b[1]) + dot(a[1], b[0]))
 
 
 def eliminate(block, rows_ref):
@@ -139,65 +64,225 @@
             rest = jnp.where((lane >= first) & (lane < first + GROUP), 0.0, rest) - change
 
 
-def factor_kernel(packed_ref, upper_ref, inverse_ref, work, panel, rows_ref):
-    size = work.shape[0]
+def back_kernel(
+    n, norming, target_ref, site_ref, center_ref,
+    high, low, turned_high, turned_low, mine, theirs, work, whole_high, whole_low,
+    upper, panel, rows_ref,
+    out_send, out_recv, back_send, back_recv,
+):
+    me = lax.axis_index("bond")
+    height, size = target_ref.shape
     blocks = size // BLOCK
-    offset = 0
-    for start in range(0, size, STRIP):
-        width = size - start
-        work[start : start + STRIP, start:] = packed_ref[:, offset : offset + width]
-        if start > 0:
-            work[start : start + STRIP, :start] = jnp.zeros((STRIP, start), jnp.float32)
-        offset += width
+    share = BLOCK // n
+    peers = [lax.rem(me + d, n) for d in range(n)]
+    barrier = pltpu.get_barrier_semaphore()
+    for peer in peers[1:]:
+        pl.semaphore_signal(barrier, inc=1, device_id={"bond": peer})
+    pl.semaphore_wait(barrier, n - 1)
+
+    def lanes_of(s):
+        return pl.ds(s * BLOCK, size - s * BLOCK)
+
+    def rows_of(s, peer):
+        return pl.ds(pl.multiple_of(s * BLOCK + peer * share, share), share)
+
+    def outward(s, d):
+        return pltpu.make_async_remote_copy(
+            src_ref=mine.at[s, peers[d], :, lanes_of(s)],
+            dst_ref=theirs.at[n - d - 1, s, :, lanes_of(s)],
+            send_sem=out_send.at[s, d],
+            recv_sem=out_recv.at[s, n - d],
+            device_id={"bond": peers[d]},
+        )
+
+    def arriving(s, d):
+        return pltpu.make_async_remote_copy(
+            src_ref=mine.at[s, peers[d], :, lanes_of(s)],
+            dst_ref=theirs.at[d - 1, s, :, lanes_of(s)],
+            send_sem=out_send.at[s, d],
+            recv_sem=out_recv.at[s, d],
+            device_id={"bond": peers[d]},
+        )
+
+    def shared(s, d):
+        here = work.at[rows_of(s, me), lanes_of(s)]
+        return pltpu.make_async_remote_copy(
+            src_ref=here,
+            dst_ref=here,
+            send_sem=back_send.at[s, d],
+            recv_sem=back_recv.at[s, n - d],
+            device_id={"bond": peers[d]},
+        )
+
+    def returning(s, d):
+        there = work.at[rows_of(s, peers[d]), lanes_of(s)]
+        return pltpu.make_async_remote_copy(
+            src_ref=there,
+            dst_ref=there,
+            send_sem=back_send.at[s, d],
+            recv_sem=back_recv.at[s, d],
+            device_id={"bond": peers[d]},
+        )
+
+    def send_out(s):
+        for d in range(1, n):
+            outward(s, d).start()
+
+    def reduce(s):
+        first = s * BLOCK
+        for d in range(1, n):
+            arriving(s, d).wait_recv()
+        value = mine[s, me, :, first:]
+        for d in range(1, n):
+            value = value + theirs[d - 1, s, :, first:]
+        work[rows_of(s, me), first:] = value
+        for d in range(1, n):
+            shared(s, d).start()
+
+    def collect(s):
+        for d in range(1, n):
+            returning(s, d).wait_recv()
+
+    slab = min(STRIP, height)
+
+    def split(i, carry):
+        span = pl.ds(pl.multiple_of(i * slab, slab), slab)
+        high[span, :], low[span, :] = halves(target_ref[span, :])
+        return carry
+
+    lax.fori_loop(0, height // slab, split, 0)
+    whole_high[...] = jnp.zeros_like(whole_high)
+    whole_low[...] = jnp.zeros_like(whole_low)
+    per = STRIP // BLOCK
+    for g in range(size // STRIP):
+        turned_high[...], turned_low[...] = halves(target_ref[:, g * STRIP : (g + 1) * STRIP].T)
+
+        def correlate(c, carry):
+            lanes = pl.ds(pl.multiple_of(c * STRIP, STRIP), STRIP)
+            value = split_dot(
+                (turned_high[...], turned_low[...]), (high[:, lanes], low[:, lanes]), ((1,), (0,))
+            )
+            for b in range(per):
+                part = value[b * BLOCK : (b + 1) * BLOCK, :]
+                for i in range(n):
+                    mine[g * per + b, i, :, lanes] = part[i * share : (i + 1) * share, :]
+            return carry
+
+        lax.fori_loop(g, size // STRIP, correlate, 0)
+        if g == 0:
+            for s in range(AHEAD):
+                send_out(s)
+    for s in range(AHEAD):
+        reduce(s)
+        send_out(s + AHEAD)
+
     row = lax.broadcasted_iota(jnp.int32, (BLOCK, BLOCK), 0)
     column = lax.broadcasted_iota(jnp.int32, (BLOCK, BLOCK), 1)
     full_column = lax.broadcasted_iota(jnp.int32, (BLOCK, size), 1)
 
     def step(k, carry):
+        for s in range(blocks):
+
+            @pl.when(k == s)
+            def _():
+                collect(s)
+
         own = pl.ds(pl.multiple_of(k * BLOCK, BLOCK), BLOCK)
-        eliminate(work[own, own], rows_ref)
+        panel[...] = jnp.where(full_column < k * BLOCK, 0.0, work[own, :])
+
+        def update(c, carry):
+            span = pl.ds(pl.multiple_of(c * STRIP, STRIP), STRIP)
+            panel[...] -= split_dot(
+                (whole_high[span, own], whole_low[span, own]),
+                (whole_high[span, :], whole_low[span, :]),
+                ((0,), (0,)),
+            )
+            return carry
+
+        lax.fori_loop(0, (k + per - 1) // per, update, 0)
+        eliminate(panel[:, own], rows_ref)
         done = rows_ref[...]
         pivots = jnp.sum(jnp.where(row == column, done, 0.0), axis=1, keepdims=True)
         scale = lax.rsqrt(pivots)
         scaled = done * scale
-        upper = jnp.where(row <= column, scaled, 0.0)
+        top = jnp.where(row <= column, scaled, 0.0)
         inverse = jnp.where(row > column, scaled, jnp.where(row == column, scale, 0.0))
-        panel[...] = product(inverse, work[own, :], ((1,), (0,)))
-        whole = panel[...]
-        upper_ref[own, :] = jnp.where(full_column >= (k + 1) * BLOCK, whole, 0.0)
-        inverse_ref[own, :] = jnp.where(full_column < k * BLOCK, whole, 0.0)
-        upper_ref[own, own] = upper
-        inverse_ref[own, own] = inverse
-        panel[:, own] = inverse
-        right = panel[...]
-
-        def update(i, carry):
-            other = pl.ds(pl.multiple_of(i * BLOCK, BLOCK), BLOCK)
-            work[other, own] = jnp.zeros((BLOCK, BLOCK), jnp.float32)
-            work[other, :] -= product(panel[:, other], right, ((0,), (0,)))
+        whole = split_dot(halves(inverse), halves(panel[...]), ((1,), (0,)))
+        upper[own, :] = jnp.where(full_column >= (k + 1) * BLOCK, whole, 0.0)
+        upper[own, own] = top
+        whole_high[:, own] = jnp.zeros((size, BLOCK), jnp.bfloat16)
+        whole_low[:, own] = jnp.zeros((size, BLOCK), jnp.bfloat16)
+        whole_high[own, :], whole_low[own, :] = halves(whole)
+        whole_high[own, own], whole_low[own, own] = halves(inverse)
+        for s in range(AHEAD, blocks):
+
+            @pl.when(k == s - AHEAD)
+            def _():
+                reduce(s)
+                if s + AHEAD < blocks:
+                    send_out(s + AHEAD)
+
+        return carry
+
+    lax.fori_loop(0, blocks, step, 0)
+    own_rows = center_ref.shape[0]
+    center_ref[...] = upper[pl.ds(pl.multiple_of(me * own_rows, own_rows), own_rows), :] / norming
+    for g in range(size // STRIP):
+        lanes = slice(g * STRIP, (g + 1) * STRIP)
+        depth = (g + 1) * STRIP
+
+        def solve(i, carry):
+            span = pl.ds(pl.multiple_of(i * slab, slab), slab)
+            value = split_dot(
+                (high[span, :depth], low[span, :depth]),
+                (whole_high[lanes, :depth], whole_low[lanes, :depth]),
+                ((1,), (1,)),
+            )
+            site_ref[span, lanes] = (value * norming).astype(jnp.bfloat16)
             return carry
 
-        lax.fori_loop(k + 1, blocks, update, 0)
-        return carry
-
-    lax.fori_loop(0, blocks, step, 0)
-
-
-def factorize(packed, size):
-    whole = jax.ShapeDtypeStruct((size, size), jnp.float32)
+        lax.fori_loop(0, height // slab, solve, 0)
+    for s in range(blocks):
+        for d in range(1, n):
+            outward(s, d).wait_send()
+            shared(s, d).wait_send()
+
+
+def back(target):
+    n = lax.axis_size("bond")
+    height, size = target.shape
+    blocks, share = size // BLOCK, BLOCK // n
+    norming = math.sqrt(size * PHYS)
+    half, full = jnp.bfloat16, jnp.float32
+    whole = pl.BlockSpec(memory_space=pltpu.VMEM)
     return pl.pallas_call(
-        factor_kernel,
-        out_shape=(whole, whole),
-        in_specs=[pl.BlockSpec(memory_space=pltpu.VMEM)],
-        out_specs=[pl.BlockSpec(memory_space=pltpu.VMEM)] * 2,
+        functools.partial(back_kernel, n, norming),
+        out_shape=(
+            jax.ShapeDtypeStruct((height, size), half),
+            jax.ShapeDtypeStruct((size // n, size), full),
+        ),
+        in_specs=[whole],
+        out_specs=[whole] * 2,
         scratch_shapes=[
-            pltpu.VMEM((size, size), jnp.float32),
-            pltpu.VMEM((BLOCK, size), jnp.float32),
-            pltpu.VMEM((BLOCK, BLOCK), jnp.float32),
-        ],
-        compiler_params=pltpu.CompilerParams(vmem_limit_bytes=40 * 2**20),
-        name="factorize",
-    )(packed)
+            pltpu.VMEM((height, size), half),
+            pltpu.VMEM((height, size), half),
+            pltpu.VMEM((STRIP, height), half),
+            pltpu.VMEM((STRIP, height), half),
+            pltpu.VMEM((blocks, n, share, size), full),
+            pltpu.VMEM((n - 1, blocks, share, size), full),
+            pltpu.VMEM((size, size), full),
+            pltpu.VMEM((size, size), half),
+            pltpu.VMEM((size, size), half),
+            pltpu.VMEM((size, size), full),
+            pltpu.VMEM((BLOCK, size), full),
+            pltpu.VMEM((BLOCK, BLOCK), full),
+        ]
+        + [pltpu.SemaphoreType.DMA((blocks, n))] * 4,
+        compiler_params=pltpu.CompilerParams(
+            collective_id=0, has_side_effects=True, vmem_limit_bytes=56 * 2**20
+        ),
+        name="back",
+    )(target)
 
 
 def minor_size(n):
@@ -565,30 +650,9 @@
         prev_right[0],
         hamiltonian[0],
     ).reshape(PHYS * own_rows, bond_width)
-    strips = [
-        jnp.dot(
-            target[:, start : start + STRIP].T,
-            target[:, start:],
-            precision=lax.Precision.HIGH,
-            preferred_element_type=jnp.float32,
-        )
-        for start in range(0, bond_width, STRIP)
-    ]
-    packed = summed(jnp.concatenate(strips, axis=1))
-    upper, inverse = factorize(packed, bond_width)
-    norming = math.sqrt(bond_width * PHYS)
-    solved = lax.dot_general(
-        target,
-        inverse,
-        (((1,), (1,)), ((), ())),
-        precision=lax.Precision.HIGH,
-        preferred_element_type=jnp.float32,
-    )
-    new_site = (solved * norming).astype(jnp.bfloat16).reshape(PHYS, own_rows, bond_width)
-    new_site = jnp.transpose(new_site, (1, 0, 2))[None]
-    offset = lax.axis_index("bond") * own_rows
-    center = lax.dynamic_slice_in_dim(upper, offset, own_rows, 0) / norming
-    return (new_site, center[None])
+    site, center = back(target)
+    site = jnp.transpose(site.reshape(PHYS, own_rows, bond_width), (1, 0, 2))
+    return (site[None], center[None])
 
 
 def solution(mesh):

time: 306 us -> 263 us (0.86)
  matrix products: 18.3 us -> 0 us
  Pallas kernels: 268 us -> 250 us
    dot_general x5 -> x0, matrix products: 18.3 us -> none  [the longest x1 9.8 us: shards(): lax.dot_general(target, inverse, (((1,), (1,)), ((), ())), precision=lax....]
    pallas_call x2 -> x1, Pallas kernels: 108 us -> 89.8 us  [back(): pl.pallas_call(functools.partial(back_kernel, n, norming), out_shape=(jax...]
    unnamed x12 -> x9, local copies, waits for them, and re-layouts: 9.21 us -> 4.51 us
where the time goes in v3:
time: 263 us
  Pallas kernels  250 us (95%)
  local copies, waits for them, and re-layouts  11.8 us (4%)
    pallas_call x1, Pallas kernels, front(): pl.pallas_call(functools.partial(front_kernel, segments, n), out_shape=ja...  160 us
    pallas_call x1, Pallas kernels, back(): pl.pallas_call(functools.partial(back_kernel, n, norming), out_shape=(jax...  89.8 us

profile of v3, /device:TPU:0, one launch (start us, length us, event | category | flops | bytes accessed | tf_op | source)
XLA Modules:
  0.0 262.9 jit_solution(4701375202738434099)
XLA Ops:
  0.6 0.0 copy-start
  0.7 1.2 copy.11
  1.9 0.6 broadcast_multiply_fusion
  2.5 1.4 mul.20.spread_ref
  3.9 0.0 copy-done
  3.9 0.0 copy-start.1
  3.9 1.9 copy.18
  5.9 0.0 copy-done.1
  5.9 1.6 copy.17
  7.5 160.0 %front.1 = f32[4,256,1024]{2,1,0:T(8,128)} custom-call(bf16[6,256,1024]{2,1,0:T(8,128)(2,1)} %bitcast.32, bf16[1024,1024]{1,0:T(8,128)(2,1)} %bitcast.34, bf16[4,256,1024]{2,1,0:T(8,128)(2,1)} %bitcast.30, bf16[6,256,1024]{2,1,0:T(8,128)(2,1)} %bitcast.33, bf16[4,1024,256]{2,1,0:T(8,128)(2,1)} %bitcast.31, bf16[1024,1024]{1,0:T(8,128)(2,1)} %bitcast.35, ...), custom_call_target="tpu_custom_call" | custom-call | tf_op jit(solution)/shard_map/front/pallas_call | solution.py:609
  167.5 89.8 %back.1 = (bf16[1024,1024]{1,0:T(8,128)(2,1)}, f32[256,1024]{1,0:T(8,128)}) custom-call(f32[1024,1024]{1,0:T(8,128)} %bitcast.29), custom_call_target="tpu_custom_call" | custom-call | tf_op jit(solution)/shard_map/back/pallas_call | solution.py:258
  257.3 0.0 copy-start.2
  257.3 4.6 %copy.16 = bf16[4,256,1024]{2,0,1:T(4,128)(2,1)} copy(bf16[4,256,1024]{2,1,0:T(8,128)(2,1)} %bitcast.37) | data formatting | bytes 4194304 | tf_op jit(solution)/shard_map/reshape | solution.py:654
  261.9 0.0 copy-done.2
  261.9 1.0 copy.20
  (1 shorter events, 0.0 us)
Async XLA Ops:
  0.6 3.3 %copy-start = (bf16[1,256,4,1024]{3,2,1,0:T(4,128)(2,1)S(1)}, bf16[1,256,4,1024]{3,2,1,0:T(4,128)(2,1)}, u32[]{:S(2)}) copy-start(bf16[1,256,4,1024]{3,2,1,0:T(4,128)(2,1)} %param.9) | copy-start | bytes 6291460
  3.9 2.0 copy-start.1
  257.3 4.6 %copy-start.2 = (f32[256,1024]{1,0:T(8,128)S(1)}, f32[256,1024]{1,0:T(8,128)}, u32[]{:S(2)}) copy-start(f32[256,1024]{1,0:T(8,128)} %get-tuple-element.5) | copy-start | bytes 3145732

commit v4 on v3

--- a/solution.py
+++ b/solution.py
@@ -15,7 +15,7 @@
 GROUP = 4
 ROWS = 8
 AHEAD = 2
-EDGES = 4
+EDGES = 8
 LEFT_ROWS = 64
 
 
@@ -67,7 +67,7 @@
 def back_kernel(
     n, norming, target_ref, site_ref, center_ref,
     high, low, turned_high, turned_low, mine, theirs, work, whole_high, whole_low,
-    upper, panel, rows_ref,
+    upper, change, panel, rows_ref,
     out_send, out_recv, back_send, back_recv,
 ):
     me = lax.axis_index("bond")
@@ -151,8 +151,6 @@
         return carry
 
     lax.fori_loop(0, height // slab, split, 0)
-    whole_high[...] = jnp.zeros_like(whole_high)
-    whole_low[...] = jnp.zeros_like(whole_low)
     per = STRIP // BLOCK
     for g in range(size // STRIP):
         turned_high[...], turned_low[...] = halves(target_ref[:, g * STRIP : (g + 1) * STRIP].T)
@@ -172,6 +170,9 @@
         if g == 0:
             for s in range(AHEAD):
                 send_out(s)
+            whole_high[...] = jnp.zeros_like(whole_high)
+            whole_low[...] = jnp.zeros_like(whole_low)
+            change[...] = jnp.zeros_like(change)
     for s in range(AHEAD):
         reduce(s)
         send_out(s + AHEAD)
@@ -180,6 +181,22 @@
     column = lax.broadcasted_iota(jnp.int32, (BLOCK, BLOCK), 1)
     full_column = lax.broadcasted_iota(jnp.int32, (BLOCK, size), 1)
 
+    def solve_strip(g):
+        lanes = slice(g * STRIP, (g + 1) * STRIP)
+        depth = (g + 1) * STRIP
+
+        def solve(i, carry):
+            span = pl.ds(pl.multiple_of(i * slab, slab), slab)
+            value = split_dot(
+                (high[span, :depth], low[span, :depth]),
+                (whole_high[lanes, :depth], whole_low[lanes, :depth]),
+                ((1,), (1,)),
+            )
+            site_ref[span, lanes] = (value * norming).astype(jnp.bfloat16)
+            return carry
+
+        lax.fori_loop(0, height // slab, solve, 0)
+
     def step(k, carry):
         for s in range(blocks):
 
@@ -188,18 +205,7 @@
                 collect(s)
 
         own = pl.ds(pl.multiple_of(k * BLOCK, BLOCK), BLOCK)
-        panel[...] = jnp.where(full_column < k * BLOCK, 0.0, work[own, :])
-
-        def update(c, carry):
-            span = pl.ds(pl.multiple_of(c * STRIP, STRIP), STRIP)
-            panel[...] -= split_dot(
-                (whole_high[span, own], whole_low[span, own]),
-                (whole_high[span, :], whole_low[span, :]),
-                ((0,), (0,)),
-            )
-            return carry
-
-        lax.fori_loop(0, (k + per - 1) // per, update, 0)
+        panel[...] = jnp.where(full_column < k * BLOCK, 0.0, work[own, :]) - change[own, :]
         eliminate(panel[:, own], rows_ref)
         done = rows_ref[...]
         pivots = jnp.sum(jnp.where(row == column, done, 0.0), axis=1, keepdims=True)
@@ -222,26 +228,44 @@
                 if s + AHEAD < blocks:
                     send_out(s + AHEAD)
 
+        def update(i, span):
+            other = pl.ds(pl.multiple_of(i * BLOCK, BLOCK), BLOCK)
+            change[other, span] = jnp.zeros((BLOCK, span.size), jnp.float32)
+            change[other, :] += split_dot(
+                (whole_high[span, other], whole_low[span, other]),
+                (whole_high[span, :], whole_low[span, :]),
+                ((0,), (0,)),
+            )
+
+        place = lax.rem(k, per)
+        for depth in range(1, per):
+
+            @pl.when((place == depth - 1) & (k + 1 < blocks))
+            def _():
+                first = (k - depth + 1) * BLOCK
+                update(k + 1, pl.ds(pl.multiple_of(first, BLOCK), depth * BLOCK))
+
+        @pl.when(place == per - 1)
+        def _():
+            span = pl.ds(pl.multiple_of((k - per + 1) * BLOCK, STRIP), STRIP)
+
+            def later(i, carry):
+                update(i, span)
+                return carry
+
+            lax.fori_loop(k + 1, blocks, later, 0)
+
+        for g in range(size // STRIP):
+
+            @pl.when(k == (g + 1) * per - 1)
+            def _():
+                solve_strip(g)
+
         return carry
 
     lax.fori_loop(0, blocks, step, 0)
     own_rows = center_ref.shape[0]
     center_ref[...] = upper[pl.ds(pl.multiple_of(me * own_rows, own_rows), own_rows), :] / norming
-    for g in range(size // STRIP):
-        lanes = slice(g * STRIP, (g + 1) * STRIP)
-        depth = (g + 1) * STRIP
-
-        def solve(i, carry):
-            span = pl.ds(pl.multiple_of(i * slab, slab), slab)
-            value = split_dot(
-                (high[span, :depth], low[span, :depth]),
-                (whole_high[lanes, :depth], whole_low[lanes, :depth]),
-                ((1,), (1,)),
-            )
-            site_ref[span, lanes] = (value * norming).astype(jnp.bfloat16)
-            return carry
-
-        lax.fori_loop(0, height // slab, solve, 0)
     for s in range(blocks):
         for d in range(1, n):
             outward(s, d).wait_send()
@@ -273,6 +297,7 @@
             pltpu.VMEM((size, size), full),
             pltpu.VMEM((size, size), half),
             pltpu.VMEM((size, size), half),
+            pltpu.VMEM((size, size), full),
             pltpu.VMEM((size, size), full),
             pltpu.VMEM((BLOCK, size), full),
             pltpu.VMEM((BLOCK, BLOCK), full),

time: 263 us -> 255 us (0.970)
  Pallas kernels: 250 us -> 242 us
    pallas_call x1, Pallas kernels: 160 us -> 155 us  [front(): pl.pallas_call(functools.partial(front_kernel, segments, n), out_shape=ja...]
    pallas_call x1, Pallas kernels: 89.8 us -> 86.7 us  [back(): pl.pallas_call(functools.partial(back_kernel, n, norming), out_shape=(jax...]
where the time goes in v4:
time: 255 us
  Pallas kernels  242 us (95%)
  local copies, waits for them, and re-layouts  11.8 us (5%)
    pallas_call x1, Pallas kernels, front(): pl.pallas_call(functools.partial(front_kernel, segments, n), out_shape=ja...  155 us
    pallas_call x1, Pallas kernels, back(): pl.pallas_call(functools.partial(back_kernel, n, norming), out_shape=(jax...  86.7 us

profile of v4, /device:TPU:0, one launch (start us, length us, event | category | flops | bytes accessed | tf_op | source)
XLA Modules:
  0.0 254.7 jit_solution(1979464072232792350)
XLA Ops:
  0.6 0.0 copy-start
  0.7 1.2 copy.11
  1.9 0.6 broadcast_multiply_fusion
  2.5 1.4 mul.20.spread_ref
  3.9 0.0 copy-done
  3.9 0.0 copy-start.1
  3.9 1.9 copy.18
  5.9 0.0 copy-done.1
  5.9 1.6 copy.17
  7.5 154.8 %front.1 = f32[4,256,1024]{2,1,0:T(8,128)} custom-call(bf16[6,256,1024]{2,1,0:T(8,128)(2,1)} %bitcast.32, bf16[1024,1024]{1,0:T(8,128)(2,1)} %bitcast.34, bf16[4,256,1024]{2,1,0:T(8,128)(2,1)} %bitcast.30, bf16[6,256,1024]{2,1,0:T(8,128)(2,1)} %bitcast.33, bf16[4,1024,256]{2,1,0:T(8,128)(2,1)} %bitcast.31, bf16[1024,1024]{1,0:T(8,128)(2,1)} %bitcast.35, ...), custom_call_target="tpu_custom_call" | custom-call | tf_op jit(solution)/shard_map/front/pallas_call | solution.py:634
  162.3 86.7 %back.1 = (bf16[1024,1024]{1,0:T(8,128)(2,1)}, f32[256,1024]{1,0:T(8,128)}) custom-call(f32[1024,1024]{1,0:T(8,128)} %bitcast.29), custom_call_target="tpu_custom_call" | custom-call | tf_op jit(solution)/shard_map/back/pallas_call | solution.py:282
  249.1 0.0 copy-start.2
  249.1 4.6 %copy.16 = bf16[4,256,1024]{2,0,1:T(4,128)(2,1)} copy(bf16[4,256,1024]{2,1,0:T(8,128)(2,1)} %bitcast.37) | data formatting | bytes 4194304 | tf_op jit(solution)/shard_map/reshape | solution.py:679
  253.7 0.0 copy-done.2
  253.7 1.0 copy.20
  (1 shorter events, 0.0 us)
Async XLA Ops:
  0.6 3.3 %copy-start = (bf16[1,256,4,1024]{3,2,1,0:T(4,128)(2,1)S(1)}, bf16[1,256,4,1024]{3,2,1,0:T(4,128)(2,1)}, u32[]{:S(2)}) copy-start(bf16[1,256,4,1024]{3,2,1,0:T(4,128)(2,1)} %param.9) | copy-start | bytes 6291460
  3.9 2.0 copy-start.1
  249.1 4.6 %copy-start.2 = (f32[256,1024]{1,0:T(8,128)S(1)}, f32[256,1024]{1,0:T(8,128)}, u32[]{:S(2)}) copy-start(f32[256,1024]{1,0:T(8,128)} %get-tuple-element.5) | copy-start | bytes 3145732

commit v5 on v4

--- a/solution.py
+++ b/solution.py
@@ -14,7 +14,7 @@
 STRIP = 256
 GROUP = 4
 ROWS = 8
-AHEAD = 2
+AHEAD = 3
 EDGES = 8
 LEFT_ROWS = 64
 
@@ -67,7 +67,7 @@
 def back_kernel(
     n, norming, target_ref, site_ref, center_ref,
     high, low, turned_high, turned_low, mine, theirs, work, whole_high, whole_low,
-    upper, change, panel, rows_ref,
+    upper, left, panel, given_high, given_low, rows_ref,
     out_send, out_recv, back_send, back_recv,
 ):
     me = lax.axis_index("bond")
@@ -81,7 +81,7 @@
     pl.semaphore_wait(barrier, n - 1)
 
     def lanes_of(s):
-        return pl.ds(s * BLOCK, size - s * BLOCK)
+        return pl.ds(0, (s + 1) * BLOCK)
 
     def rows_of(s, peer):
         return pl.ds(pl.multiple_of(s * BLOCK + peer * share, share), share)
@@ -129,13 +129,13 @@
             outward(s, d).start()
 
     def reduce(s):
-        first = s * BLOCK
+        last = (s + 1) * BLOCK
         for d in range(1, n):
             arriving(s, d).wait_recv()
-        value = mine[s, me, :, first:]
+        value = mine[s, me, :, :last]
         for d in range(1, n):
-            value = value + theirs[d - 1, s, :, first:]
-        work[rows_of(s, me), first:] = value
+            value = value + theirs[d - 1, s, :, :last]
+        work[rows_of(s, me), :last] = value
         for d in range(1, n):
             shared(s, d).start()
 
@@ -166,16 +166,16 @@
                     mine[g * per + b, i, :, lanes] = part[i * share : (i + 1) * share, :]
             return carry
 
-        lax.fori_loop(g, size // STRIP, correlate, 0)
-        if g == 0:
-            for s in range(AHEAD):
-                send_out(s)
-            whole_high[...] = jnp.zeros_like(whole_high)
-            whole_low[...] = jnp.zeros_like(whole_low)
-            change[...] = jnp.zeros_like(change)
-    for s in range(AHEAD):
+        lax.fori_loop(0, g + 1, correlate, 0)
+        for s in range(g * per, min((g + 1) * per, AHEAD)):
+            send_out(s)
+    whole_high[...] = jnp.zeros_like(whole_high)
+    whole_low[...] = jnp.zeros_like(whole_low)
+    left[...] = jnp.zeros_like(left)
+    for s in range(min(AHEAD, blocks)):
         reduce(s)
-        send_out(s + AHEAD)
+        if s + AHEAD < blocks:
+            send_out(s + AHEAD)
 
     row = lax.broadcasted_iota(jnp.int32, (BLOCK, BLOCK), 0)
     column = lax.broadcasted_iota(jnp.int32, (BLOCK, BLOCK), 1)
@@ -203,58 +203,53 @@
             @pl.when(k == s)
             def _():
                 collect(s)
+                if s + AHEAD < blocks:
+                    reduce(s + AHEAD)
+                if s + 2 * AHEAD < blocks:
+                    send_out(s + 2 * AHEAD)
 
         own = pl.ds(pl.multiple_of(k * BLOCK, BLOCK), BLOCK)
-        panel[...] = jnp.where(full_column < k * BLOCK, 0.0, work[own, :]) - change[own, :]
-        eliminate(panel[:, own], rows_ref)
+        given_high[...], given_low[...] = halves(
+            jnp.where(full_column < k * BLOCK, work[own, :], 0.0)
+        )
+
+        def reach(c, carry):
+            span = pl.ds(pl.multiple_of(c * STRIP, STRIP), STRIP)
+            left[:, span] = split_dot(
+                (given_high[...], given_low[...]),
+                (whole_high[span, :], whole_low[span, :]),
+                ((1,), (1,)),
+            )
+            return carry
+
+        chunks = (k + per - 1) // per
+        lax.fori_loop(0, chunks, reach, 0)
+        given_high[...], given_low[...] = halves(left[...])
+        given = (given_high[...], given_low[...])
+        eliminate(work[own, own] - split_dot(given, given, ((1,), (1,))), rows_ref)
+        panel[...] = jnp.zeros_like(panel)
+
+        def gather(c, carry):
+            span = pl.ds(pl.multiple_of(c * STRIP, STRIP), STRIP)
+            panel[...] += split_dot(
+                (given_high[:, span], given_low[:, span]),
+                (whole_high[span, :], whole_low[span, :]),
+                ((1,), (0,)),
+            )
+            return carry
+
+        lax.fori_loop(0, chunks, gather, 0)
         done = rows_ref[...]
         pivots = jnp.sum(jnp.where(row == column, done, 0.0), axis=1, keepdims=True)
         scale = lax.rsqrt(pivots)
         scaled = done * scale
         top = jnp.where(row <= column, scaled, 0.0)
         inverse = jnp.where(row > column, scaled, jnp.where(row == column, scale, 0.0))
-        whole = split_dot(halves(inverse), halves(panel[...]), ((1,), (0,)))
-        upper[own, :] = jnp.where(full_column >= (k + 1) * BLOCK, whole, 0.0)
-        upper[own, own] = top
-        whole_high[:, own] = jnp.zeros((size, BLOCK), jnp.bfloat16)
-        whole_low[:, own] = jnp.zeros((size, BLOCK), jnp.bfloat16)
+        whole = split_dot(halves(-inverse), halves(panel[...]), ((1,), (0,)))
         whole_high[own, :], whole_low[own, :] = halves(whole)
         whole_high[own, own], whole_low[own, own] = halves(inverse)
-        for s in range(AHEAD, blocks):
-
-            @pl.when(k == s - AHEAD)
-            def _():
-                reduce(s)
-                if s + AHEAD < blocks:
-                    send_out(s + AHEAD)
-
-        def update(i, span):
-            other = pl.ds(pl.multiple_of(i * BLOCK, BLOCK), BLOCK)
-            change[other, span] = jnp.zeros((BLOCK, span.size), jnp.float32)
-            change[other, :] += split_dot(
-                (whole_high[span, other], whole_low[span, other]),
-                (whole_high[span, :], whole_low[span, :]),
-                ((0,), (0,)),
-            )
-
-        place = lax.rem(k, per)
-        for depth in range(1, per):
-
-            @pl.when((place == depth - 1) & (k + 1 < blocks))
-            def _():
-                first = (k - depth + 1) * BLOCK
-                update(k + 1, pl.ds(pl.multiple_of(first, BLOCK), depth * BLOCK))
-
-        @pl.when(place == per - 1)
-        def _():
-            span = pl.ds(pl.multiple_of((k - per + 1) * BLOCK, STRIP), STRIP)
-
-            def later(i, carry):
-                update(i, span)
-                return carry
-
-            lax.fori_loop(k + 1, blocks, later, 0)
-
+        upper[:, own] = left[...].T
+        upper[own, own] = top
         for g in range(size // STRIP):
 
             @pl.when(k == (g + 1) * per - 1)
@@ -298,8 +293,10 @@
             pltpu.VMEM((size, size), half),
             pltpu.VMEM((size, size), half),
             pltpu.VMEM((size, size), full),
-            pltpu.VMEM((size, size), full),
             pltpu.VMEM((BLOCK, size), full),
+            pltpu.VMEM((BLOCK, size), full),
+            pltpu.VMEM((BLOCK, size), half),
+            pltpu.VMEM((BLOCK, size), half),
             pltpu.VMEM((BLOCK, BLOCK), full),
         ]
         + [pltpu.SemaphoreType.DMA((blocks, n))] * 4,

time: 255 us -> 255 us (level)
  no operation moved by 1% of the time
where the time goes in v5:
time: 255 us
  Pallas kernels  242 us (95%)
  local copies, waits for them, and re-layouts  11.8 us (5%)
    pallas_call x1, Pallas kernels, front(): pl.pallas_call(functools.partial(front_kernel, segments, n), out_shape=ja...  155 us
    pallas_call x1, Pallas kernels, back(): pl.pallas_call(functools.partial(back_kernel, n, norming), out_shape=(jax...  86.9 us

profile of v5, /device:TPU:0, one launch (start us, length us, event | category | flops | bytes accessed | tf_op | source)
XLA Modules:
  0.0 254.9 jit_solution(3831069210977441308)
XLA Ops:
  0.6 0.0 copy-start
  0.7 1.2 copy.11
  1.9 0.6 broadcast_multiply_fusion
  2.5 1.4 mul.20.spread_ref
  3.9 0.0 copy-done
  3.9 0.0 copy-start.1
  3.9 1.9 copy.18
  5.9 0.0 copy-done.1
  5.9 1.6 copy.17
  7.5 154.8 %front.1 = f32[4,256,1024]{2,1,0:T(8,128)} custom-call(bf16[6,256,1024]{2,1,0:T(8,128)(2,1)} %bitcast.32, bf16[1024,1024]{1,0:T(8,128)(2,1)} %bitcast.34, bf16[4,256,1024]{2,1,0:T(8,128)(2,1)} %bitcast.30, bf16[6,256,1024]{2,1,0:T(8,128)(2,1)} %bitcast.33, bf16[4,1024,256]{2,1,0:T(8,128)(2,1)} %bitcast.31, bf16[1024,1024]{1,0:T(8,128)(2,1)} %bitcast.35, ...), custom_call_target="tpu_custom_call" | custom-call | tf_op jit(solution)/shard_map/front/pallas_call | solution.py:631
  162.3 86.9 %back.1 = (bf16[1024,1024]{1,0:T(8,128)(2,1)}, f32[256,1024]{1,0:T(8,128)}) custom-call(f32[1024,1024]{1,0:T(8,128)} %bitcast.29), custom_call_target="tpu_custom_call" | custom-call | tf_op jit(solution)/shard_map/back/pallas_call | solution.py:277
  249.3 0.0 copy-start.2
  249.3 4.6 %copy.16 = bf16[4,256,1024]{2,0,1:T(4,128)(2,1)} copy(bf16[4,256,1024]{2,1,0:T(8,128)(2,1)} %bitcast.37) | data formatting | bytes 4194304 | tf_op jit(solution)/shard_map/reshape | solution.py:676
  253.9 0.0 copy-done.2
  253.9 1.0 copy.20
  (1 shorter events, 0.0 us)
Async XLA Ops:
  0.6 3.3 %copy-start = (bf16[1,256,4,1024]{3,2,1,0:T(4,128)(2,1)S(1)}, bf16[1,256,4,1024]{3,2,1,0:T(4,128)(2,1)}, u32[]{:S(2)}) copy-start(bf16[1,256,4,1024]{3,2,1,0:T(4,128)(2,1)} %param.9) | copy-start | bytes 6291460
  3.9 2.0 copy-start.1
  249.3 4.6 %copy-start.2 = (f32[256,1024]{1,0:T(8,128)S(1)}, f32[256,1024]{1,0:T(8,128)}, u32[]{:S(2)}) copy-start(f32[256,1024]{1,0:T(8,128)} %get-tuple-element.5) | copy-start | bytes 3145732

commit v6 on v5

--- a/solution.py
+++ b/solution.py
@@ -13,6 +13,7 @@
 BLOCK = 128
 STRIP = 256
 GROUP = 4
+PIECE = 64
 ROWS = 8
 AHEAD = 3
 EDGES = 8
@@ -31,42 +32,68 @@
     return dot(a[0], b[0]) + (dot(a[0], b[1]) + dot(a[1], b[0]))
 
 
-def eliminate(block, rows_ref):
-    size = block.shape[0]
+def eliminate(block, base, rows_ref):
+    height, size = block.shape
     lane = lax.broadcasted_iota(jnp.int32, (1, size), 1)
     rest = block
     top = 0
-    for first in range(0, size, GROUP):
+    for first in range(0, height, GROUP):
         start = first // 8 * 8
         rest, top = rest[start - top :], start
         at = first - top
+        pivot = base + first
         rows = [rest[at + q : at + q + 1, :] for q in range(GROUP)]
         columns = [
-            jnp.broadcast_to(rest[:, first + q : first + q + 1], rest.shape) for q in range(GROUP)
+            jnp.broadcast_to(rest[:, pivot + q : pivot + q + 1], rest.shape) for q in range(GROUP)
         ]
         small = [[columns[r][at + p : at + p + 1, :] for r in range(GROUP)] for p in range(GROUP)]
         change = None
         for q in range(GROUP):
-            rows_ref[pl.ds(first + q, 1), :] = rows[q]
+            rows_ref[pl.ds(pivot + q, 1), :] = rows[q]
             inverse = 1.0 / small[q][q]
-            lead = jnp.where(lane == first + q, 1.0, rows[q])
+            lead = jnp.where(lane == pivot + q, 1.0, rows[q])
             for p in range(q + 1, GROUP):
                 factor = small[q][p] * inverse
                 for r in range(p, GROUP):
                     small[p][r] = small[p][r] - factor * small[q][r]
-                rows[p] = jnp.where(lane == first + q, 0.0, rows[p]) - factor * lead
+                rows[p] = jnp.where(lane == pivot + q, 0.0, rows[p]) - factor * lead
                 columns[p] = columns[p] - factor * columns[q]
-            if first + GROUP < size:
-                lead = jnp.where((lane > first + q) & (lane < first + GROUP), 0.0, lead)
+            if first + GROUP < height:
+                lead = jnp.where((lane > pivot + q) & (lane < pivot + GROUP), 0.0, lead)
                 term = columns[q] * (inverse * lead)
                 change = term if change is None else change + term
-        if first + GROUP < size:
-            rest = jnp.where((lane >= first) & (lane < first + GROUP), 0.0, rest) - change
+        if first + GROUP < height:
+            rest = jnp.where((lane >= pivot) & (lane < pivot + GROUP), 0.0, rest) - change
+
+
+def factor_tile(block, rows_ref):
+    size = block.shape[0]
+    row = lax.broadcasted_iota(jnp.int32, (PIECE, size), 0)
+    column = lax.broadcasted_iota(jnp.int32, (PIECE, size), 1)
+    tops, inverses = [], []
+    for base in range(0, size, PIECE):
+        eliminate(block[:PIECE], base, rows_ref)
+        done = rows_ref[base : base + PIECE, :]
+        diagonal = column == row + base
+        scale = lax.rsqrt(jnp.sum(jnp.where(diagonal, done, 0.0), axis=1, keepdims=True))
+        scaled = done * scale
+        upper = jnp.where(column >= row + base, scaled, 0.0)
+        inverse = jnp.where(column < row + base, scaled, jnp.where(diagonal, scale, 0.0))
+        tops.append(upper)
+        inverses.append(inverse)
+        if base + PIECE < size:
+            right = jnp.where(column >= base + PIECE, scaled, inverse)
+            change = split_dot(halves(scaled), halves(right), ((0,), (0,)))
+            below = block[PIECE:]
+            inside = lax.broadcasted_iota(jnp.int32, below.shape, 1)
+            inside = (inside >= base) & (inside < base + PIECE)
+            block = jnp.where(inside, 0.0, below) - change[base + PIECE :]
+    return jnp.concatenate(tops, axis=0), jnp.concatenate(inverses, axis=0)
 
 
 def back_kernel(
     n, norming, target_ref, site_ref, center_ref,
-    high, low, turned_high, turned_low, mine, theirs, work, whole_high, whole_low,
+    turned, mine, theirs, work, whole_high, whole_low,
     upper, left, panel, given_high, given_low, rows_ref,
     out_send, out_recv, back_send, back_recv,
 ):
@@ -145,21 +172,13 @@
 
     slab = min(STRIP, height)
 
-    def split(i, carry):
-        span = pl.ds(pl.multiple_of(i * slab, slab), slab)
-        high[span, :], low[span, :] = halves(target_ref[span, :])
-        return carry
-
-    lax.fori_loop(0, height // slab, split, 0)
     per = STRIP // BLOCK
     for g in range(size // STRIP):
-        turned_high[...], turned_low[...] = halves(target_ref[:, g * STRIP : (g + 1) * STRIP].T)
+        turned[...] = target_ref[:, g * STRIP : (g + 1) * STRIP].T
 
         def correlate(c, carry):
             lanes = pl.ds(pl.multiple_of(c * STRIP, STRIP), STRIP)
-            value = split_dot(
-                (turned_high[...], turned_low[...]), (high[:, lanes], low[:, lanes]), ((1,), (0,))
-            )
+            value = jnp.dot(turned[...], target_ref[:, lanes], preferred_element_type=jnp.float32)
             for b in range(per):
                 part = value[b * BLOCK : (b + 1) * BLOCK, :]
                 for i in range(n):
@@ -177,8 +196,6 @@
         if s + AHEAD < blocks:
             send_out(s + AHEAD)
 
-    row = lax.broadcasted_iota(jnp.int32, (BLOCK, BLOCK), 0)
-    column = lax.broadcasted_iota(jnp.int32, (BLOCK, BLOCK), 1)
     full_column = lax.broadcasted_iota(jnp.int32, (BLOCK, size), 1)
 
     def solve_strip(g):
@@ -187,10 +204,17 @@
 
         def solve(i, carry):
             span = pl.ds(pl.multiple_of(i * slab, slab), slab)
-            value = split_dot(
-                (high[span, :depth], low[span, :depth]),
-                (whole_high[lanes, :depth], whole_low[lanes, :depth]),
-                ((1,), (1,)),
+            given = target_ref[span, :depth]
+            value = lax.dot_general(
+                given,
+                whole_high[lanes, :depth],
+                (((1,), (1,)), ((), ())),
+                preferred_element_type=jnp.float32,
+            ) + lax.dot_general(
+                given,
+                whole_low[lanes, :depth],
+                (((1,), (1,)), ((), ())),
+                preferred_element_type=jnp.float32,
             )
             site_ref[span, lanes] = (value * norming).astype(jnp.bfloat16)
             return carry
@@ -213,38 +237,34 @@
             jnp.where(full_column < k * BLOCK, work[own, :], 0.0)
         )
 
-        def reach(c, carry):
-            span = pl.ds(pl.multiple_of(c * STRIP, STRIP), STRIP)
-            left[:, span] = split_dot(
-                (given_high[...], given_low[...]),
-                (whole_high[span, :], whole_low[span, :]),
-                ((1,), (1,)),
-            )
-            return carry
-
-        chunks = (k + per - 1) // per
-        lax.fori_loop(0, chunks, reach, 0)
+        for c in range(size // STRIP):
+
+            @pl.when(c * per < k)
+            def _():
+                span, depth = slice(c * STRIP, (c + 1) * STRIP), (c + 1) * STRIP
+                left[:, span] = split_dot(
+                    (given_high[:, :depth], given_low[:, :depth]),
+                    (whole_high[span, :depth], whole_low[span, :depth]),
+                    ((1,), (1,)),
+                )
+
         given_high[...], given_low[...] = halves(left[...])
         given = (given_high[...], given_low[...])
-        eliminate(work[own, own] - split_dot(given, given, ((1,), (1,))), rows_ref)
         panel[...] = jnp.zeros_like(panel)
-
-        def gather(c, carry):
-            span = pl.ds(pl.multiple_of(c * STRIP, STRIP), STRIP)
-            panel[...] += split_dot(
-                (given_high[:, span], given_low[:, span]),
-                (whole_high[span, :], whole_low[span, :]),
-                ((1,), (0,)),
-            )
-            return carry
-
-        lax.fori_loop(0, chunks, gather, 0)
-        done = rows_ref[...]
-        pivots = jnp.sum(jnp.where(row == column, done, 0.0), axis=1, keepdims=True)
-        scale = lax.rsqrt(pivots)
-        scaled = done * scale
-        top = jnp.where(row <= column, scaled, 0.0)
-        inverse = jnp.where(row > column, scaled, jnp.where(row == column, scale, 0.0))
+        for c in range(size // STRIP):
+
+            @pl.when(c * per < k)
+            def _():
+                span, depth = slice(c * STRIP, (c + 1) * STRIP), (c + 1) * STRIP
+                panel[:, :depth] += split_dot(
+                    (given_high[:, span], given_low[:, span]),
+                    (whole_high[span, :depth], whole_low[span, :depth]),
+                    ((1,), (0,)),
+                )
+
+        top, inverse = factor_tile(
+            work[own, own] - split_dot(given, given, ((1,), (1,))), rows_ref
+        )
         whole = split_dot(halves(-inverse), halves(panel[...]), ((1,), (0,)))
         whole_high[own, :], whole_low[own, :] = halves(whole)
         whole_high[own, own], whole_low[own, own] = halves(inverse)
@@ -283,9 +303,6 @@
         in_specs=[whole],
         out_specs=[whole] * 2,
         scratch_shapes=[
-            pltpu.VMEM((height, size), half),
-            pltpu.VMEM((height, size), half),
-            pltpu.VMEM((STRIP, height), half),
             pltpu.VMEM((STRIP, height), half),
             pltpu.VMEM((blocks, n, share, size), full),
             pltpu.VMEM((n - 1, blocks, share, size), full),
@@ -320,6 +337,7 @@
     segments, n, left_ref, prev_left_ref, current_ref, right_ref,
     prev_site_ref, prev_right_ref, spread_ref, target_ref,
     left, current, right, prev_left, partial_out, partial_in, projected, mixture, outgoing, incoming,
+    total,
     left_send, left_recv, prev_send, prev_recv, major_send, major_recv, minor_send, minor_recv,
     relay_send, relay_recv, right_send, right_recv, partial_send, partial_recv,
     target_send, target_recv, local_sem,
@@ -592,19 +610,22 @@
             sends.append(flow)
 
         def own_part(s, lanes, value):
-            target_ref[s, :, lanes] = value
+            total[s, :, lanes] = value
 
         products(0, j, own_part)
     for j, (first, width) in enumerate(spans):
         for d in range(1, p):
             target_flow(d, j, d).wait_recv()
-            lanes = slice(first, first + width)
-
-            def add(s, carry):
-                target_ref[s, :, lanes] += incoming[d - 1, s, :, lanes].astype(jnp.float32)
-                return carry
-
-            lax.fori_loop(0, PHYS, add, 0)
+        lanes = slice(first, first + width)
+
+        def add(s, carry):
+            value = total[s, :, lanes]
+            for d in range(1, p):
+                value = value + incoming[d - 1, s, :, lanes].astype(jnp.float32)
+            target_ref[s, :, lanes] = value.astype(jnp.bfloat16)
+            return carry
+
+        lax.fori_loop(0, PHYS, add, 0)
     for flow in sends:
         flow.wait_send()
 
@@ -630,7 +651,7 @@
 
     return pl.pallas_call(
         functools.partial(front_kernel, segments, n),
-        out_shape=jax.ShapeDtypeStruct((PHYS, own, bond), full),
+        out_shape=jax.ShapeDtypeStruct((PHYS, own, bond), low),
         in_specs=[there] * 4 + [whole] * 3,
         out_specs=whole,
         scratch_shapes=[
@@ -644,6 +665,7 @@
             pltpu.VMEM((PHYS, tall, MPOB * wide), low),
             pltpu.VMEM((max(p - 1, 1), PHYS, own, bond), low),
             pltpu.VMEM((max(p - 1, 1), PHYS, own, bond), low),
+            pltpu.VMEM((PHYS, own, bond), full),
         ]
         + pairs(p, own // rows)
         + pairs(1)

time: 255 us -> 247 us (0.969)
  Pallas kernels: 242 us -> 234 us
    pallas_call x1, Pallas kernels: 86.9 us -> 79.7 us  [back(): pl.pallas_call(functools.partial(back_kernel, n, norming), out_shape=(jax...]
where the time goes in v6:
time: 247 us
  Pallas kernels  234 us (95%)
  local copies, waits for them, and re-layouts  11.8 us (5%)
    pallas_call x1, Pallas kernels, front(): pl.pallas_call(functools.partial(front_kernel, segments, n), out_shape=ja...  154 us
    pallas_call x1, Pallas kernels, back(): pl.pallas_call(functools.partial(back_kernel, n, norming), out_shape=(jax...  79.7 us

profile of v6, /device:TPU:0, one launch (start us, length us, event | category | flops | bytes accessed | tf_op | source)
XLA Modules:
  0.0 247.2 jit_solution(18149933851341001610)
XLA Ops:
  0.6 0.0 copy-start
  0.7 1.2 copy.11
  1.9 0.6 broadcast_multiply_fusion
  2.5 1.4 mul.20.spread_ref
  3.9 0.0 copy-done
  3.9 0.0 copy-start.1
  3.9 1.9 copy.18
  5.9 0.0 copy-done.1
  5.9 1.6 copy.17
  7.5 154.4 %front.1 = bf16[4,256,1024]{2,1,0:T(8,128)(2,1)} custom-call(bf16[6,256,1024]{2,1,0:T(8,128)(2,1)} %bitcast.32, bf16[1024,1024]{1,0:T(8,128)(2,1)} %bitcast.36, bf16[4,256,1024]{2,1,0:T(8,128)(2,1)} %bitcast.30, bf16[6,256,1024]{2,1,0:T(8,128)(2,1)} %bitcast.33, bf16[4,1024,256]{2,1,0:T(8,128)(2,1)} %bitcast.31, bf16[1024,1024]{1,0:T(8,128)(2,1)} %bitcast.37, ...), custom_call_target="tpu_custom_call" | custom-call | tf_op jit(solution)/shard_map/front/pallas_call | solution.py:652
  161.9 79.7 %back.1 = (bf16[1024,1024]{1,0:T(8,128)(2,1)}, f32[256,1024]{1,0:T(8,128)}) custom-call(bf16[1024,1024]{1,0:T(8,128)(2,1)} %bitcast.29), custom_call_target="tpu_custom_call" | custom-call | tf_op jit(solution)/shard_map/back/pallas_call | solution.py:297
  241.6 0.0 copy-start.2
  241.6 4.6 %copy.16 = bf16[4,256,1024]{2,0,1:T(4,128)(2,1)} copy(bf16[4,256,1024]{2,1,0:T(8,128)(2,1)} %bitcast.35) | data formatting | bytes 4194304 | tf_op jit(solution)/shard_map/reshape | solution.py:698
  246.2 0.0 copy-done.2
  246.2 1.0 copy.20
  (1 shorter events, 0.0 us)
Async XLA Ops:
  0.6 3.3 %copy-start = (bf16[1,256,4,1024]{3,2,1,0:T(4,128)(2,1)S(1)}, bf16[1,256,4,1024]{3,2,1,0:T(4,128)(2,1)}, u32[]{:S(2)}) copy-start(bf16[1,256,4,1024]{3,2,1,0:T(4,128)(2,1)} %param.9) | copy-start | bytes 6291460
  3.9 2.0 copy-start.1
  241.6 4.6 %copy-start.2 = (f32[256,1024]{1,0:T(8,128)S(1)}, f32[256,1024]{1,0:T(8,128)}, u32[]{:S(2)}) copy-start(f32[256,1024]{1,0:T(8,128)} %get-tuple-element.5) | copy-start | bytes 3145732

commit v7 on v6

--- a/solution.py
+++ b/solution.py
@@ -12,7 +12,7 @@
 MPOB = 6
 BLOCK = 128
 STRIP = 256
-GROUP = 4
+GROUP = 8
 PIECE = 64
 ROWS = 8
 AHEAD = 3
@@ -170,8 +170,6 @@
         for d in range(1, n):
             returning(s, d).wait_recv()
 
-    slab = min(STRIP, height)
-
     per = STRIP // BLOCK
     for g in range(size // STRIP):
         turned[...] = target_ref[:, g * STRIP : (g + 1) * STRIP].T
@@ -198,28 +196,14 @@
 
     full_column = lax.broadcasted_iota(jnp.int32, (BLOCK, size), 1)
 
-    def solve_strip(g):
-        lanes = slice(g * STRIP, (g + 1) * STRIP)
-        depth = (g + 1) * STRIP
-
-        def solve(i, carry):
-            span = pl.ds(pl.multiple_of(i * slab, slab), slab)
-            given = target_ref[span, :depth]
-            value = lax.dot_general(
-                given,
-                whole_high[lanes, :depth],
-                (((1,), (1,)), ((), ())),
-                preferred_element_type=jnp.float32,
-            ) + lax.dot_general(
-                given,
-                whole_low[lanes, :depth],
-                (((1,), (1,)), ((), ())),
-                preferred_element_type=jnp.float32,
-            )
-            site_ref[span, lanes] = (value * norming).astype(jnp.bfloat16)
-            return carry
-
-        lax.fori_loop(0, height // slab, solve, 0)
+    def solve_block(k):
+        own = pl.ds(pl.multiple_of(k * BLOCK, BLOCK), BLOCK)
+        dims = (((1,), (1,)), ((), ()))
+        target = target_ref[...]
+        value = lax.dot_general(
+            target, whole_high[own, :], dims, preferred_element_type=jnp.float32
+        ) + lax.dot_general(target, whole_low[own, :], dims, preferred_element_type=jnp.float32)
+        site_ref[:, own] = (value * norming).astype(jnp.bfloat16)
 
     def step(k, carry):
         for s in range(blocks):
@@ -250,35 +234,20 @@
 
         given_high[...], given_low[...] = halves(left[...])
         given = (given_high[...], given_low[...])
-        panel[...] = jnp.zeros_like(panel)
-        for c in range(size // STRIP):
-
-            @pl.when(c * per < k)
-            def _():
-                span, depth = slice(c * STRIP, (c + 1) * STRIP), (c + 1) * STRIP
-                panel[:, :depth] += split_dot(
-                    (given_high[:, span], given_low[:, span]),
-                    (whole_high[span, :depth], whole_low[span, :depth]),
-                    ((1,), (0,)),
-                )
-
+        panel[...] = split_dot(given, (whole_high[...], whole_low[...]), ((1,), (0,)))
+        solve_block(jnp.maximum(k - 1, 0))
+        upper[:, own] = left[...].T
         top, inverse = factor_tile(
             work[own, own] - split_dot(given, given, ((1,), (1,))), rows_ref
         )
         whole = split_dot(halves(-inverse), halves(panel[...]), ((1,), (0,)))
         whole_high[own, :], whole_low[own, :] = halves(whole)
         whole_high[own, own], whole_low[own, own] = halves(inverse)
-        upper[:, own] = left[...].T
         upper[own, own] = top
-        for g in range(size // STRIP):
-
-            @pl.when(k == (g + 1) * per - 1)
-            def _():
-                solve_strip(g)
-
         return carry
 
     lax.fori_loop(0, blocks, step, 0)
+    solve_block(blocks - 1)
     own_rows = center_ref.shape[0]
     center_ref[...] = upper[pl.ds(pl.multiple_of(me * own_rows, own_rows), own_rows), :] / norming
     for s in range(blocks):
@@ -318,7 +287,7 @@
         ]
         + [pltpu.SemaphoreType.DMA((blocks, n))] * 4,
         compiler_params=pltpu.CompilerParams(
-            collective_id=0, has_side_effects=True, vmem_limit_bytes=56 * 2**20
+            collective_id=0, has_side_effects=True, vmem_limit_bytes=36 * 2**20
         ),
         name="back",
     )(target)

time: 247 us -> 240 us (0.972)
  Pallas kernels: 234 us -> 227 us
    pallas_call x1, Pallas kernels: 79.7 us -> 72.2 us  [back(): pl.pallas_call(functools.partial(back_kernel, n, norming), out_shape=(jax...]
where the time goes in v7:
time: 240 us
  Pallas kernels  227 us (95%)
  local copies, waits for them, and re-layouts  11.7 us (5%)
    pallas_call x1, Pallas kernels, front(): pl.pallas_call(functools.partial(front_kernel, segments, n), out_shape=ja...  154 us
    pallas_call x1, Pallas kernels, back(): pl.pallas_call(functools.partial(back_kernel, n, norming), out_shape=(jax...  72.2 us
    unnamed x9, local copies, waits for them, and re-layouts  6.11 us

profile of v7, /device:TPU:0, one launch (start us, length us, event | category | flops | bytes accessed | tf_op | source)
XLA Modules:
  0.0 239.6 jit_solution(13210310249110886063)
XLA Ops:
  0.6 0.0 copy-start.1
  0.7 1.2 copy.11
  1.9 0.6 broadcast_multiply_fusion
  2.5 1.4 mul.20.spread_ref
  3.9 0.0 copy-done.1
  3.9 0.0 copy-start.2
  3.9 1.9 copy.18
  5.9 0.0 copy-done.2
  5.9 1.6 copy.17
  7.5 154.4 %front.1 = bf16[4,256,1024]{2,1,0:T(8,128)(2,1)} custom-call(bf16[6,256,1024]{2,1,0:T(8,128)(2,1)} %bitcast.34, bf16[1024,1024]{1,0:T(8,128)(2,1)} %bitcast.37, bf16[4,256,1024]{2,1,0:T(8,128)(2,1)} %bitcast.32, bf16[6,256,1024]{2,1,0:T(8,128)(2,1)} %bitcast.35, bf16[4,1024,256]{2,1,0:T(8,128)(2,1)} %bitcast.33, bf16[1024,1024]{1,0:T(8,128)(2,1)} %bitcast.38, ...), custom_call_target="tpu_custom_call" | custom-call | tf_op jit(solution)/shard_map/front/pallas_call | solution.py:621
  161.9 0.0 copy-start
  161.9 1.6 copy-done
  163.5 72.2 %back.1 = (bf16[1024,1024]{1,0:T(8,128)(2,1)S(1)}, f32[256,1024]{1,0:T(8,128)S(1)}) custom-call(bf16[1024,1024]{1,0:T(8,128)(2,1)S(1)} %bitcast.29), custom_call_target="tpu_custom_call" | custom-call | tf_op jit(solution)/shard_map/back/pallas_call | solution.py:266
  235.7 2.9 %copy.16 = bf16[4,256,1024]{2,0,1:T(4,128)(2,1)} copy(bf16[4,256,1024]{2,1,0:T(8,128)(2,1)S(1)} %bitcast.30) | data formatting | bytes 4194304 | tf_op jit(solution)/shard_map/reshape | solution.py:667
  238.6 1.0 copy.20
  (1 shorter events, 0.0 us)
Async XLA Ops:
  0.6 3.3 %copy-start.1 = (bf16[1,256,4,1024]{3,2,1,0:T(4,128)(2,1)S(1)}, bf16[1,256,4,1024]{3,2,1,0:T(4,128)(2,1)}, u32[]{:S(2)}) copy-start(bf16[1,256,4,1024]{3,2,1,0:T(4,128)(2,1)} %param.9) | copy-start | bytes 6291460
  3.9 2.0 copy-start.2
  161.9 1.6 copy-start

commit v8 on v7

--- a/solution.py
+++ b/solution.py
@@ -302,11 +302,44 @@
     return [(j * unit, unit) for j in range(EDGES)]
 
 
+def spread_coupling(coupling):
+    pair, side = PHYS * ROWS, MPOB * PHYS * ROWS
+
+    def grid(height, width):
+        shape = (height, width)
+        return [lax.broadcasted_iota(jnp.int32, shape, axis) for axis in range(2)]
+
+    def hot(mask):
+        return jnp.where(mask, 1.0, 0.0).astype(jnp.bfloat16)
+
+    total = None
+    for u in range(MPOB):
+        row, column = grid(side, MPOB * MPOB)
+        offset = row - pair * (column - u * MPOB)
+        picked = jnp.dot(
+            hot((offset >= 0) & (offset < pair)), coupling, preferred_element_type=jnp.float32
+        )
+        row, column = grid(side, PHYS * PHYS)
+        offset = (row & (pair - 1)) * PHYS - ROWS * (column & (PHYS * PHYS - PHYS))
+        kept = jnp.where((offset >= 0) & (offset < ROWS * PHYS), picked, 0.0)
+        row, column = grid(PHYS * PHYS, side)
+        offset = column - u * pair - ROWS * (row & (PHYS - 1))
+        term = jnp.dot(
+            kept.astype(jnp.bfloat16),
+            hot((offset >= 0) & (offset < ROWS)),
+            preferred_element_type=jnp.float32,
+        )
+        total = term if total is None else total + term
+    row, column = grid(side, side)
+    same = (row & (ROWS - 1)) == (column & (ROWS - 1))
+    return jnp.where(same, total, 0.0).astype(jnp.bfloat16)
+
+
 def front_kernel(
     segments, n, left_ref, prev_left_ref, current_ref, right_ref,
-    prev_site_ref, prev_right_ref, spread_ref, target_ref,
+    prev_site_ref, prev_right_ref, coupling_ref, target_ref,
     left, current, right, prev_left, partial_out, partial_in, projected, mixture, outgoing, incoming,
-    total,
+    total, spread_ref,
     left_send, left_recv, prev_send, prev_recv, major_send, major_recv, minor_send, minor_recv,
     relay_send, relay_recv, right_send, right_recv, partial_send, partial_recv,
     target_send, target_recv, local_sem,
@@ -409,6 +442,8 @@
     for one in locals_:
         one.start()
 
+    spread_ref[...] = spread_coupling(coupling_ref[...])
+
     for h in range(2):
         for dm in range(1, p):
             landed = current.at[:, current_rows(dm, 0, h), :]
@@ -608,9 +643,6 @@
     rows = min(LEFT_ROWS, own)
     edges = len(edge_spans(bond))
     side = MPOB * PHYS * ROWS
-    diagonal = jnp.eye(ROWS, dtype=coupling.dtype)
-    turned = jnp.transpose(coupling, (1, 2, 0, 3))
-    spread = turned[:, :, None, :, :, None] * diagonal[None, None, :, None, None, :]
     low, full = jnp.bfloat16, jnp.float32
     whole = pl.BlockSpec(memory_space=pltpu.VMEM)
     there = pl.BlockSpec(memory_space=pl.ANY)
@@ -635,6 +667,7 @@
             pltpu.VMEM((max(p - 1, 1), PHYS, own, bond), low),
             pltpu.VMEM((max(p - 1, 1), PHYS, own, bond), low),
             pltpu.VMEM((PHYS, own, bond), full),
+            pltpu.VMEM((side, side), low),
         ]
         + pairs(p, own // rows)
         + pairs(1)
@@ -646,10 +679,10 @@
         + pairs(p, edges)
         + [pltpu.SemaphoreType.DMA((2,))],
         compiler_params=pltpu.CompilerParams(
-            collective_id=1, has_side_effects=True, vmem_limit_bytes=56 * 2**20
+            collective_id=1, has_side_effects=True, vmem_limit_bytes=49 * 2**20
         ),
         name="front",
-    )(left, prev_left, current, right, prev_site, prev_right, spread.reshape(side, side))
+    )(left, prev_left, current, right, prev_site, prev_right, coupling)
 
 
 def shards(left_env, prev_left, cur_site, prev_site, hamiltonian, right_env, prev_right):
@@ -661,7 +694,7 @@
         jnp.transpose(right_env[0], (1, 0, 2)),
         jnp.transpose(prev_site[0], (1, 0, 2)),
         prev_right[0],
-        hamiltonian[0],
+        hamiltonian[0].reshape(MPOB * MPOB, PHYS * PHYS),
     ).reshape(PHYS * own_rows, bond_width)
     site, center = back(target)
     site = jnp.transpose(site.reshape(PHYS, own_rows, bond_width), (1, 0, 2))

time: 240 us -> 237 us (0.988)
    unnamed x9 -> x7, local copies, waits for them, and re-layouts: 6.11 us -> 7.01 us
where the time goes in v8:
time: 237 us
  Pallas kernels  225 us (95%)
  local copies, waits for them, and re-layouts  11 us (5%)
    pallas_call x1, Pallas kernels, front(): pl.pallas_call(functools.partial(front_kernel, segments, n), out_shape=ja...  153 us
    pallas_call x1, Pallas kernels, back(): pl.pallas_call(functools.partial(back_kernel, n, norming), out_shape=(jax...  72.2 us
    unnamed x7, local copies, waits for them, and re-layouts  7.01 us

profile of v8, /device:TPU:0, one launch (start us, length us, event | category | flops | bytes accessed | tf_op | source)
XLA Modules:
  0.0 237.0 jit_solution(10912926901531153157)
XLA Ops:
  0.6 1.0 copy.18
  1.6 0.1 reshape.12.coupling_ref
  1.7 0.0 copy-start.1
  1.7 3.7 %copy.25 = bf16[1,256,4,1024]{3,1,2,0:T(8,128)(2,1)} copy(bf16[1,256,4,1024]{3,2,1,0:T(4,128)(2,1)} %param.9) | data formatting | bytes 4194304 | tf_op args[2]
  5.4 0.0 copy-done.1
  5.4 0.0 copy-start
  5.4 1.6 copy.24
  7.1 0.7 copy-done
  7.8 153.1 %front.1 = bf16[4,256,1024]{2,1,0:T(8,128)(2,1)S(1)} custom-call(bf16[6,256,1024]{2,1,0:T(8,128)(2,1)} %bitcast.32, bf16[1024,1024]{1,0:T(8,128)(2,1)S(1)} %bitcast.28, bf16[4,256,1024]{2,1,0:T(8,128)(2,1)} %bitcast.30, bf16[6,256,1024]{2,1,0:T(8,128)(2,1)} %bitcast.33, bf16[4,1024,256]{2,1,0:T(8,128)(2,1)} %bitcast.31, bf16[1024,1024]{1,0:T(8,128)(2,1)} %bitcast.35, ...), custom_call_target="tpu_custom_call" | custom-call | tf_op jit(solution)/shard_map/front/pallas_call | solution.py:653
  160.9 72.2 %back.1 = (bf16[1024,1024]{1,0:T(8,128)(2,1)S(1)}, f32[256,1024]{1,0:T(8,128)S(1)}) custom-call(bf16[1024,1024]{1,0:T(8,128)(2,1)S(1)} %bitcast.26), custom_call_target="tpu_custom_call" | custom-call | tf_op jit(solution)/shard_map/back/pallas_call | solution.py:266
  233.1 2.9 %copy.23 = bf16[4,256,1024]{2,0,1:T(4,128)(2,1)} copy(bf16[4,256,1024]{2,1,0:T(8,128)(2,1)S(1)} %bitcast.27) | data formatting | bytes 4194304 | tf_op jit(solution)/shard_map/reshape | solution.py:700
  236.1 1.0 copy.27
Async XLA Ops:
  1.7 3.7 %copy-start.1 = (bf16[1,1024,4,256]{3,2,1,0:T(4,128)(2,1)S(1)}, bf16[1,1024,4,256]{3,2,1,0:T(4,128)(2,1)}, u32[]{:S(2)}) copy-start(bf16[1,1024,4,256]{3,2,1,0:T(4,128)(2,1)} %param.10) | copy-start | bytes 6291460
  5.4 2.3 copy-start

commit v9 on v7

--- a/solution.py
+++ b/solution.py
@@ -302,11 +302,41 @@
     return [(j * unit, unit) for j in range(EDGES)]
 
 
+def spread_coupling(coupling):
+    pair, side, table = PHYS * ROWS, MPOB * PHYS * ROWS, MPOB * PHYS * PHYS
+
+    def grid(height, width):
+        shape = (height, width)
+        return [lax.broadcasted_iota(jnp.int32, shape, axis) for axis in range(2)]
+
+    def within(offset, size):
+        return (offset >= 0) & (offset < size)
+
+    row, column = grid(side, MPOB)
+    hot = jnp.where(within(row - pair * column, pair), 1.0, 0.0).astype(jnp.bfloat16)
+    picked = lax.dot_general(
+        hot, coupling, (((1,), (1,)), ((), ())), preferred_element_type=jnp.float32
+    )
+    row, column = grid(side, table)
+    offset = (row & (pair - 1)) * PHYS - ROWS * (column & (PHYS * PHYS - PHYS))
+    kept = jnp.where(within(offset, ROWS * PHYS), picked, 0.0).astype(jnp.bfloat16)
+    row, column = grid(table, side)
+    first = (row & (PHYS - 1)) * ROWS
+    same_u = within(row * pair - column * (PHYS * PHYS) + (column & (pair - 1)) * (PHYS * PHYS)
+                    - (row & (PHYS * PHYS - 1)) * pair, 1)
+    same_t = within((column & (pair - 1)) - first, ROWS)
+    hot = jnp.where(same_u & same_t, 1.0, 0.0).astype(jnp.bfloat16)
+    total = jnp.dot(kept, hot, preferred_element_type=jnp.float32)
+    row, column = grid(side, side)
+    same = (row & (ROWS - 1)) == (column & (ROWS - 1))
+    return jnp.where(same, total, 0.0).astype(jnp.bfloat16)
+
+
 def front_kernel(
     segments, n, left_ref, prev_left_ref, current_ref, right_ref,
-    prev_site_ref, prev_right_ref, spread_ref, target_ref,
+    prev_site_ref, prev_right_ref, coupling_ref, target_ref,
     left, current, right, prev_left, partial_out, partial_in, projected, mixture, outgoing, incoming,
-    total,
+    total, spread_ref,
     left_send, left_recv, prev_send, prev_recv, major_send, major_recv, minor_send, minor_recv,
     relay_send, relay_recv, right_send, right_recv, partial_send, partial_recv,
     target_send, target_recv, local_sem,
@@ -409,6 +439,8 @@
     for one in locals_:
         one.start()
 
+    spread_ref[...] = spread_coupling(coupling_ref[...])
+
     for h in range(2):
         for dm in range(1, p):
             landed = current.at[:, current_rows(dm, 0, h), :]
@@ -608,9 +640,6 @@
     rows = min(LEFT_ROWS, own)
     edges = len(edge_spans(bond))
     side = MPOB * PHYS * ROWS
-    diagonal = jnp.eye(ROWS, dtype=coupling.dtype)
-    turned = jnp.transpose(coupling, (1, 2, 0, 3))
-    spread = turned[:, :, None, :, :, None] * diagonal[None, None, :, None, None, :]
     low, full = jnp.bfloat16, jnp.float32
     whole = pl.BlockSpec(memory_space=pltpu.VMEM)
     there = pl.BlockSpec(memory_space=pl.ANY)
@@ -635,6 +664,7 @@
             pltpu.VMEM((max(p - 1, 1), PHYS, own, bond), low),
             pltpu.VMEM((max(p - 1, 1), PHYS, own, bond), low),
             pltpu.VMEM((PHYS, own, bond), full),
+            pltpu.VMEM((side, side), low),
         ]
         + pairs(p, own // rows)
         + pairs(1)
@@ -646,10 +676,10 @@
         + pairs(p, edges)
         + [pltpu.SemaphoreType.DMA((2,))],
         compiler_params=pltpu.CompilerParams(
-            collective_id=1, has_side_effects=True, vmem_limit_bytes=56 * 2**20
+            collective_id=1, has_side_effects=True, vmem_limit_bytes=49 * 2**20
         ),
         name="front",
-    )(left, prev_left, current, right, prev_site, prev_right, spread.reshape(side, side))
+    )(left, prev_left, current, right, prev_site, prev_right, coupling)
 
 
 def shards(left_env, prev_left, cur_site, prev_site, hamiltonian, right_env, prev_right):
@@ -661,7 +691,7 @@
         jnp.transpose(right_env[0], (1, 0, 2)),
         jnp.transpose(prev_site[0], (1, 0, 2)),
         prev_right[0],
-        hamiltonian[0],
+        jnp.transpose(hamiltonian[0], (0, 2, 3, 1)).reshape(MPOB * PHYS * PHYS, MPOB),
     ).reshape(PHYS * own_rows, bond_width)
     site, center = back(target)
     site = jnp.transpose(site.reshape(PHYS, own_rows, bond_width), (1, 0, 2))

time: 240 us -> 236 us (0.983)
  no operation moved by 1% of the time
where the time goes in v9:
time: 236 us
  Pallas kernels  225 us (95%)
  local copies, waits for them, and re-layouts  9.95 us (4%)
    pallas_call x1, Pallas kernels, front(): pl.pallas_call(functools.partial(front_kernel, segments, n), out_shape=ja...  153 us
    pallas_call x1, Pallas kernels, back(): pl.pallas_call(functools.partial(back_kernel, n, norming), out_shape=(jax...  72.2 us
    unnamed x9, local copies, waits for them, and re-layouts  7.01 us

profile of v9, /device:TPU:0, one launch (start us, length us, event | category | flops | bytes accessed | tf_op | source)
XLA Modules:
  0.0 235.9 jit_solution(16853820346592960107)
XLA Ops:
  0.6 0.0 copy-start.2
  0.6 3.7 %copy.17 = bf16[1,256,4,1024]{3,1,2,0:T(8,128)(2,1)} copy(bf16[1,256,4,1024]{3,2,1,0:T(4,128)(2,1)} %param.9) | data formatting | bytes 4194304 | tf_op args[2]
  4.3 0.0 copy-done.2
  4.3 0.0 copy-start
  4.3 0.0 copy-start.1
  4.3 1.6 copy.16
  5.9 0.7 copy-done
  6.7 0.0 copy-done.1
  6.7 153.1 %front.1 = bf16[4,256,1024]{2,1,0:T(8,128)(2,1)S(1)} custom-call(bf16[6,256,1024]{2,1,0:T(8,128)(2,1)} %bitcast.38, bf16[1024,1024]{1,0:T(8,128)(2,1)S(1)} %bitcast.32, bf16[4,256,1024]{2,1,0:T(8,128)(2,1)} %bitcast.36, bf16[6,256,1024]{2,1,0:T(8,128)(2,1)} %bitcast.39, bf16[4,1024,256]{2,1,0:T(8,128)(2,1)} %bitcast.37, bf16[1024,1024]{1,0:T(8,128)(2,1)} %bitcast.40, ...), custom_call_target="tpu_custom_call" | custom-call | tf_op jit(solution)/shard_map/front/pallas_call | solution.py:650
  159.8 72.2 %back.1 = (bf16[1024,1024]{1,0:T(8,128)(2,1)S(1)}, f32[256,1024]{1,0:T(8,128)S(1)}) custom-call(bf16[1024,1024]{1,0:T(8,128)(2,1)S(1)} %bitcast.31), custom_call_target="tpu_custom_call" | custom-call | tf_op jit(solution)/shard_map/back/pallas_call | solution.py:266
  232.0 2.9 %copy.15 = bf16[4,256,1024]{2,0,1:T(4,128)(2,1)} copy(bf16[4,256,1024]{2,1,0:T(8,128)(2,1)S(1)} %bitcast.33) | data formatting | bytes 4194304 | tf_op jit(solution)/shard_map/reshape | solution.py:697
  234.9 1.0 copy.19
Async XLA Ops:
  0.6 3.7 %copy-start.2 = (bf16[1,1024,4,256]{3,2,1,0:T(4,128)(2,1)S(1)}, bf16[1,1024,4,256]{3,2,1,0:T(4,128)(2,1)}, u32[]{:S(2)}) copy-start(bf16[1,1024,4,256]{3,2,1,0:T(4,128)(2,1)} %param.10) | copy-start | bytes 6291460
  4.3 2.3 copy-start
  4.3 2.3 copy-start.1
